TPU v7x, 512 devices: a whole 4x8x8 slice. The times are simulated.
512 devices in a mesh: depth: 16 (over y, core), slab: 32 (over z, x).
Axes of the slice: x: 4, y: 8, z: 8, core: 2. Of those that a mesh axis runs over, the one named last changes fastest.
Arguments:
- slabs: float32 [16, 32, 4, 256, 256], P('depth', 'slab'), as said below
- incident: float32 [16, 8192, 256], P('depth', 'slab'), may hold values from -6 to 6
Outputs:
- down_field: float32 [16, 8192, 256], P('depth', 'slab')
- reflected: float32 [16, 8192, 256], P('depth', 'slab')
Inputs may be any that keep to these rules, and one draw needn't show every extreme that they name: Reflection blocks have spectral norm below one half; transmission blocks have spectral norm below 2, and every star product of consecutive slabs within a group has reflection blocks of norm below one.
All inputs are finite; a program needn't handle non-finite values.
Results may differ from a plain program's by a relative error of at most 0.0003.
Values sent between devices are 32-bit elements; how exact they have to be, the bound alone decides.
A program may use at most 64 MiB of HBM per device.

v0:
```python
import jax
import jax.numpy as jnp
from jax import lax
from jax.sharding import PartitionSpec as P


def partner(block, axis, stride):
    count = lax.axis_size(axis)
    route = []
    for low in range(count):
        high = low | 1 << stride
        if high != low and high < count:
            route += [(low, high), (high, low)]
    return lax.ppermute(block, axis, route)


def from_behind(block, axis, distance):
    devices = range(lax.axis_size(axis))
    route = [(i - distance, i) for i in devices if i - distance in devices]
    return lax.ppermute(block, axis, route)


def matmul(left, right):
    return jnp.dot(left, right, precision=lax.Precision.HIGHEST, preferred_element_type=jnp.float32)


def times_transpose(rows, matrix):
    return lax.dot_general(
        rows,
        matrix,
        (((1,), (1,)), ((), ())),
        precision=lax.Precision.HIGHEST,
        preferred_element_type=jnp.float32,
    )


def transpose_times(left, right):
    return lax.dot_general(
        left,
        right,
        (((0,), (0,)), ((), ())),
        precision=lax.Precision.HIGHEST,
        preferred_element_type=jnp.float32,
    )


def block_solve(system, right):
    extent = system.shape[0]
    if extent <= 128:
        normal_matrix = transpose_times(system, system)
        factor = jnp.linalg.cholesky(normal_matrix)
        return jax.scipy.linalg.cho_solve((factor, True), transpose_times(system, right))
    middle = extent // 2
    top_left = system[:middle, :middle]
    top_right = system[:middle, middle:]
    bottom_left = system[middle:, :middle]
    bottom_right = system[middle:, middle:]
    upper_solved = block_solve(top_left, jnp.concatenate([top_right, right[:middle]], axis=1))
    coupling = upper_solved[:, : extent - middle]
    partial_top = upper_solved[:, extent - middle :]
    schur = bottom_right - matmul(bottom_left, coupling)
    lower_part = block_solve(schur, right[middle:] - matmul(bottom_left, partial_top))
    upper_part = partial_top - matmul(coupling, lower_part)
    return jnp.concatenate([upper_part, lower_part], axis=0)


def star(upper, lower):
    order = upper.shape[1]
    refl_a, trans_a, back_a, up_a = (upper[0], upper[1], upper[2], upper[3])
    refl_b, trans_b, back_b, up_b = (lower[0], lower[1], lower[2], lower[3])
    eye = jnp.eye(order, dtype=jnp.float32)
    system = eye - matmul(back_a, refl_b)
    right = jnp.concatenate([trans_a, matmul(back_a, up_b)], axis=1)
    solved = block_solve(system, right)
    first = solved[:, :order]
    second = solved[:, order:]
    refl = refl_a + matmul(up_a, matmul(refl_b, first))
    trans = matmul(trans_b, first)
    back = back_b + matmul(trans_b, second)
    upward = matmul(up_a, up_b + matmul(refl_b, second))
    return jnp.stack([refl, trans, back, upward])


def shards(slabs, incident):
    own = slabs[0, 0]
    levels = lax.axis_size("slab").bit_length() - 1
    position = lax.axis_index("slab")
    merged = own
    for level in range(levels):
        other = partner(merged, "slab", level)
        is_lower = position // 2**level % 2 == 1
        upper = jnp.where(is_lower, other, merged)
        lower = jnp.where(is_lower, merged, other)
        merged = star(upper, lower)
    refl = merged[0]
    trans = merged[1]
    injected = incident[0]

    def handover(turn, field):
        leaving = times_transpose(field, trans)
        return injected + from_behind(leaving, "depth", 1)

    field = lax.fori_loop(0, lax.axis_size("depth") - 1, handover, injected)
    bounced = times_transpose(field, refl)
    return (field[None], bounced[None])


def solution(mesh):
    placed = (P("depth", "slab", None, None, None), P("depth", "slab", None))
    return jax.shard_map(
        shards,
        mesh=mesh,
        in_specs=placed,
        out_specs=(P("depth", "slab", None), P("depth", "slab", None)),
        check_vma=False,
    )
```

profile of v0, /device:TPU:34, one launch (start us, length us, event | category | flops | bytes accessed | tf_op | source)
XLA Modules:
  0.0 621.9 jit_solution(9659316249198694367)
XLA Ops:
  2.2 2.4 collective-permute-start.1
  4.7 24.4 %collective-permute-done.1 = f32[4,256,256]{1,2,0:T(8,128)} collective-permute-done((f32[4,256,256]{1,2,0:T(8,128)S(1)}, f32[4,256,256]{1,2,0:T(8,128)}, u32[]{:S(2)}, u32[]{:S(2)}) %collective-permute-start.1) | collective-permute-done | bytes 1048608 | tf_op jit(solution)/shard_map/ppermute | solution.py:14
  31.7 11.7 %cholesky.164 = f32[128,128]{1,0:T(8,128)S(1)} custom-call(f32[128,128]{1,0:T(8,128)S(1)} %fusion.156), custom_call_target="Cholesky" | custom-call | tf_op jit(solution)/shard_map/jit(cholesky)/cholesky | solution.py:51
  44.8 9.8 %custom-call.20 = f32[1,128,128]{1,2,0:T(8,128)S(1)} custom-call(f32[1,128,128]{2,1,0:T(8,128)S(1)} %fusion.97), custom_call_target="InvertDiagBlocksLowerTriangular" | custom-call | tf_op jit(solution)/shard_map/jit(_cho_solve)/triangular_solve | solution.py:52
  57.3 12.2 %cholesky.175 = f32[128,128]{1,0:T(8,128)S(1)} custom-call(f32[128,128]{1,0:T(8,128)S(1)} %fusion.151), custom_call_target="Cholesky" | custom-call | tf_op jit(solution)/shard_map/jit(cholesky)/cholesky | solution.py:51
  70.8 10.4 %custom-call.21 = f32[1,128,128]{1,2,0:T(8,128)} custom-call(f32[1,128,128]{2,1,0:T(8,128)S(1)} %fusion.98), custom_call_target="InvertDiagBlocksLowerTriangular" | custom-call | tf_op jit(solution)/shard_map/jit(_cho_solve)/triangular_solve | solution.py:52
  86.8 4.2 collective-permute-start.2
  91.0 23.3 %collective-permute-done.2 = f32[4,256,256]{1,2,0:T(8,128)} collective-permute-done((f32[4,256,256]{1,2,0:T(8,128)S(1)}, f32[4,256,256]{1,2,0:T(8,128)}, u32[]{:S(2)}, u32[]{:S(2)}) %collective-permute-start.2) | collective-permute-done | bytes 1048608 | tf_op jit(solution)/shard_map/ppermute | solution.py:14
  117.0 11.7 %cholesky.186 = f32[128,128]{1,0:T(8,128)S(1)} custom-call(f32[128,128]{1,0:T(8,128)S(1)} %fusion.146), custom_call_target="Cholesky" | custom-call | tf_op jit(solution)/shard_map/jit(cholesky)/cholesky | solution.py:51
  130.1 9.8 %custom-call.22 = f32[1,128,128]{1,2,0:T(8,128)S(1)} custom-call(f32[1,128,128]{2,1,0:T(8,128)S(1)} %fusion.99), custom_call_target="InvertDiagBlocksLowerTriangular" | custom-call | tf_op jit(solution)/shard_map/jit(_cho_solve)/triangular_solve | solution.py:52
  142.6 11.9 %cholesky.197 = f32[128,128]{1,0:T(8,128)S(1)} custom-call(f32[128,128]{1,0:T(8,128)S(1)} %fusion.141), custom_call_target="Cholesky" | custom-call | tf_op jit(solution)/shard_map/jit(cholesky)/cholesky | solution.py:51
  155.9 10.4 %custom-call.23 = f32[1,128,128]{1,2,0:T(8,128)} custom-call(f32[1,128,128]{2,1,0:T(8,128)S(1)} %fusion.100), custom_call_target="InvertDiagBlocksLowerTriangular" | custom-call | tf_op jit(solution)/shard_map/jit(_cho_solve)/triangular_solve | solution.py:52
  171.8 4.7 collective-permute-start.3
  176.6 21.1 %collective-permute-done.3 = f32[4,256,256]{1,2,0:T(8,128)} collective-permute-done((f32[4,256,256]{1,2,0:T(8,128)S(1)}, f32[4,256,256]{1,2,0:T(8,128)}, u32[]{:S(2)}, u32[]{:S(2)}) %collective-permute-start.3) | collective-permute-done | bytes 1048608 | tf_op jit(solution)/shard_map/ppermute | solution.py:14
  200.4 11.7 %cholesky.208 = f32[128,128]{1,0:T(8,128)S(1)} custom-call(f32[128,128]{1,0:T(8,128)S(1)} %fusion.136), custom_call_target="Cholesky" | custom-call | tf_op jit(solution)/shard_map/jit(cholesky)/cholesky | solution.py:51
  213.4 9.8 %custom-call.24 = f32[1,128,128]{1,2,0:T(8,128)S(1)} custom-call(f32[1,128,128]{2,1,0:T(8,128)S(1)} %fusion.101), custom_call_target="InvertDiagBlocksLowerTriangular" | custom-call | tf_op jit(solution)/shard_map/jit(_cho_solve)/triangular_solve | solution.py:52
  225.9 11.9 %cholesky.219 = f32[128,128]{1,0:T(8,128)S(1)} custom-call(f32[128,128]{1,0:T(8,128)S(1)} %fusion.131), custom_call_target="Cholesky" | custom-call | tf_op jit(solution)/shard_map/jit(cholesky)/cholesky | solution.py:51
  239.1 10.4 %custom-call.25 = f32[1,128,128]{1,2,0:T(8,128)} custom-call(f32[1,128,128]{2,1,0:T(8,128)S(1)} %fusion.102), custom_call_target="InvertDiagBlocksLowerTriangular" | custom-call | tf_op jit(solution)/shard_map/jit(_cho_solve)/triangular_solve | solution.py:52
  255.1 6.3 %collective-permute-start.4 = (f32[4,256,256]{1,2,0:T(8,128)S(1)}, f32[4,256,256]{1,2,0:T(8,128)}, u32[]{:S(2)}, u32[]{:S(2)}) collective-permute-start(f32[4,256,256]{1,2,0:T(8,128)S(1)} %pad_maximum_fusion.2), channel_id=1, source_target_pairs={{0,8},{8,0},{1,9},{9,1},{2,10},{10,2},{3,11},{11,3},{4,12},{12,4},... | collective-permute-start | bytes 3145736 | tf_op jit(solution)/shard_map/ppermute | solution.py:14
  261.5 43.2 %collective-permute-done.4 = f32[4,256,256]{1,2,0:T(8,128)} collective-permute-done((f32[4,256,256]{1,2,0:T(8,128)S(1)}, f32[4,256,256]{1,2,0:T(8,128)}, u32[]{:S(2)}, u32[]{:S(2)}) %collective-permute-start.4) | collective-permute-done | bytes 1048608 | tf_op jit(solution)/shard_map/ppermute | solution.py:14
  307.4 11.7 %cholesky.230 = f32[128,128]{1,0:T(8,128)S(1)} custom-call(f32[128,128]{1,0:T(8,128)S(1)} %fusion.126), custom_call_target="Cholesky" | custom-call | tf_op jit(solution)/shard_map/jit(cholesky)/cholesky | solution.py:51
  320.5 9.8 %custom-call.26 = f32[1,128,128]{1,2,0:T(8,128)S(1)} custom-call(f32[1,128,128]{2,1,0:T(8,128)S(1)} %fusion.103), custom_call_target="InvertDiagBlocksLowerTriangular" | custom-call | tf_op jit(solution)/shard_map/jit(_cho_solve)/triangular_solve | solution.py:52
  333.0 12.1 %cholesky.241 = f32[128,128]{1,0:T(8,128)S(1)} custom-call(f32[128,128]{1,0:T(8,128)S(1)} %fusion.121), custom_call_target="Cholesky" | custom-call | tf_op jit(solution)/shard_map/jit(cholesky)/cholesky | solution.py:51
  346.4 10.4 %custom-call.27 = f32[1,128,128]{1,2,0:T(8,128)} custom-call(f32[1,128,128]{2,1,0:T(8,128)S(1)} %fusion.104), custom_call_target="InvertDiagBlocksLowerTriangular" | custom-call | tf_op jit(solution)/shard_map/jit(_cho_solve)/triangular_solve | solution.py:52
  362.4 8.6 %collective-permute-start.5 = (f32[4,256,256]{1,2,0:T(8,128)S(1)}, f32[4,256,256]{1,2,0:T(8,128)}, u32[]{:S(2)}, u32[]{:S(2)}) collective-permute-start(f32[4,256,256]{1,2,0:T(8,128)S(1)} %pad_maximum_fusion.3), channel_id=1, source_target_pairs={{0,16},{16,0},{1,17},{17,1},{2,18},{18,2},{3,19},{19,3},{4,20},{20... | collective-permute-start | bytes 3145736 | tf_op jit(solution)/shard_map/ppermute | solution.py:14
  371.1 45.1 %collective-permute-done.5 = f32[4,256,256]{1,2,0:T(8,128)} collective-permute-done((f32[4,256,256]{1,2,0:T(8,128)S(1)}, f32[4,256,256]{1,2,0:T(8,128)}, u32[]{:S(2)}, u32[]{:S(2)}) %collective-permute-start.5) | collective-permute-done | bytes 1048608 | tf_op jit(solution)/shard_map/ppermute | solution.py:14
  420.1 12.5 %cholesky.252 = f32[128,128]{1,0:T(8,128)S(1)} custom-call(f32[128,128]{1,0:T(8,128)} %fusion.116), custom_call_target="Cholesky" | custom-call | tf_op jit(solution)/shard_map/jit(cholesky)/cholesky | solution.py:51
  434.0 9.8 %custom-call.28 = f32[1,128,128]{1,2,0:T(8,128)S(1)} custom-call(f32[1,128,128]{2,1,0:T(8,128)S(1)} %fusion.105), custom_call_target="InvertDiagBlocksLowerTriangular" | custom-call | tf_op jit(solution)/shard_map/jit(_cho_solve)/triangular_solve | solution.py:52
  450.1 12.7 %cholesky.263 = f32[128,128]{1,0:T(8,128)S(1)} custom-call(f32[128,128]{1,0:T(8,128)} %fusion.111), custom_call_target="Cholesky" | custom-call | tf_op jit(solution)/shard_map/jit(cholesky)/cholesky | solution.py:51
  465.0 10.6 %custom-call.29 = f32[1,128,128]{1,2,0:T(8,128)S(1)} custom-call(f32[1,128,128]{2,1,0:T(8,128)} %fusion.106), custom_call_target="InvertDiagBlocksLowerTriangular" | custom-call | tf_op jit(solution)/shard_map/jit(_cho_solve)/triangular_solve | solution.py:52
  480.0 140.6 %while.10 = (s32[]{:T(128)}, f32[256,256]{1,0:T(8,128)S(1)}, f32[256,256]{1,0:T(8,128)S(1)}, f32[256,256]{1,0:T(8,128)S(1)}, s32[]{:T(128)}) while((s32[]{:T(128)}, f32[256,256]{1,0:T(8,128)S(1)}, f32[256,256]{1,0:T(8,128)S(1)}, f32[256,256]{1,0:T(8,128)S(1)}, s32[]{:T(128)}) %tuple.33), condition=%wide.region_3.7_spmd, body=%wide.region_2.6_spmd.sunk | while | flops 201392128 | bytes 2621541 | solution.py:103
  482.3 7.0 %collective-permute-done = f32[256,256]{1,0:T(8,128)S(1)} collective-permute-done((f32[256,256]{1,0:T(8,128)S(1)}, f32[256,256]{1,0:T(8,128)S(1)}, u32[]{:S(2)}, u32[]{:S(2)}) %collective-permute-start) | collective-permute-done | bytes 262176 | tf_op jit(solution)/shard_map/while/body/eval_jaxpr/ppermute | solution.py:20
  489.8 1.9 collective-permute-start
  491.7 7.0 %collective-permute-done = f32[256,256]{1,0:T(8,128)S(1)} collective-permute-done((f32[256,256]{1,0:T(8,128)S(1)}, f32[256,256]{1,0:T(8,128)S(1)}, u32[]{:S(2)}, u32[]{:S(2)}) %collective-permute-start) | collective-permute-done | bytes 262176 | tf_op jit(solution)/shard_map/while/body/eval_jaxpr/ppermute | solution.py:20
  499.2 1.9 collective-permute-start
  501.1 7.0 %collective-permute-done = f32[256,256]{1,0:T(8,128)S(1)} collective-permute-done((f32[256,256]{1,0:T(8,128)S(1)}, f32[256,256]{1,0:T(8,128)S(1)}, u32[]{:S(2)}, u32[]{:S(2)}) %collective-permute-start) | collective-permute-done | bytes 262176 | tf_op jit(solution)/shard_map/while/body/eval_jaxpr/ppermute | solution.py:20
  510.5 7.0 %collective-permute-done = f32[256,256]{1,0:T(8,128)S(1)} collective-permute-done((f32[256,256]{1,0:T(8,128)S(1)}, f32[256,256]{1,0:T(8,128)S(1)}, u32[]{:S(2)}, u32[]{:S(2)}) %collective-permute-start) | collective-permute-done | bytes 262176 | tf_op jit(solution)/shard_map/while/body/eval_jaxpr/ppermute | solution.py:20
  519.8 7.0 %collective-permute-done = f32[256,256]{1,0:T(8,128)S(1)} collective-permute-done((f32[256,256]{1,0:T(8,128)S(1)}, f32[256,256]{1,0:T(8,128)S(1)}, u32[]{:S(2)}, u32[]{:S(2)}) %collective-permute-start) | collective-permute-done | bytes 262176 | tf_op jit(solution)/shard_map/while/body/eval_jaxpr/ppermute | solution.py:20
  529.2 7.0 %collective-permute-done = f32[256,256]{1,0:T(8,128)S(1)} collective-permute-done((f32[256,256]{1,0:T(8,128)S(1)}, f32[256,256]{1,0:T(8,128)S(1)}, u32[]{:S(2)}, u32[]{:S(2)}) %collective-permute-start) | collective-permute-done | bytes 262176 | tf_op jit(solution)/shard_map/while/body/eval_jaxpr/ppermute | solution.py:20
  538.6 7.0 %collective-permute-done = f32[256,256]{1,0:T(8,128)S(1)} collective-permute-done((f32[256,256]{1,0:T(8,128)S(1)}, f32[256,256]{1,0:T(8,128)S(1)}, u32[]{:S(2)}, u32[]{:S(2)}) %collective-permute-start) | collective-permute-done | bytes 262176 | tf_op jit(solution)/shard_map/while/body/eval_jaxpr/ppermute | solution.py:20
  548.0 7.0 %collective-permute-done = f32[256,256]{1,0:T(8,128)S(1)} collective-permute-done((f32[256,256]{1,0:T(8,128)S(1)}, f32[256,256]{1,0:T(8,128)S(1)}, u32[]{:S(2)}, u32[]{:S(2)}) %collective-permute-start) | collective-permute-done | bytes 262176 | tf_op jit(solution)/shard_map/while/body/eval_jaxpr/ppermute | solution.py:20
  557.3 7.0 %collective-permute-done = f32[256,256]{1,0:T(8,128)S(1)} collective-permute-done((f32[256,256]{1,0:T(8,128)S(1)}, f32[256,256]{1,0:T(8,128)S(1)}, u32[]{:S(2)}, u32[]{:S(2)}) %collective-permute-start) | collective-permute-done | bytes 262176 | tf_op jit(solution)/shard_map/while/body/eval_jaxpr/ppermute | solution.py:20
  566.7 7.0 %collective-permute-done = f32[256,256]{1,0:T(8,128)S(1)} collective-permute-done((f32[256,256]{1,0:T(8,128)S(1)}, f32[256,256]{1,0:T(8,128)S(1)}, u32[]{:S(2)}, u32[]{:S(2)}) %collective-permute-start) | collective-permute-done | bytes 262176 | tf_op jit(solution)/shard_map/while/body/eval_jaxpr/ppermute | solution.py:20
  576.1 7.0 %collective-permute-done = f32[256,256]{1,0:T(8,128)S(1)} collective-permute-done((f32[256,256]{1,0:T(8,128)S(1)}, f32[256,256]{1,0:T(8,128)S(1)}, u32[]{:S(2)}, u32[]{:S(2)}) %collective-permute-start) | collective-permute-done | bytes 262176 | tf_op jit(solution)/shard_map/while/body/eval_jaxpr/ppermute | solution.py:20
  585.4 7.0 %collective-permute-done = f32[256,256]{1,0:T(8,128)S(1)} collective-permute-done((f32[256,256]{1,0:T(8,128)S(1)}, f32[256,256]{1,0:T(8,128)S(1)}, u32[]{:S(2)}, u32[]{:S(2)}) %collective-permute-start) | collective-permute-done | bytes 262176 | tf_op jit(solution)/shard_map/while/body/eval_jaxpr/ppermute | solution.py:20
  594.8 7.0 %collective-permute-done = f32[256,256]{1,0:T(8,128)S(1)} collective-permute-done((f32[256,256]{1,0:T(8,128)S(1)}, f32[256,256]{1,0:T(8,128)S(1)}, u32[]{:S(2)}, u32[]{:S(2)}) %collective-permute-start) | collective-permute-done | bytes 262176 | tf_op jit(solution)/shard_map/while/body/eval_jaxpr/ppermute | solution.py:20
  604.2 7.0 %collective-permute-done = f32[256,256]{1,0:T(8,128)S(1)} collective-permute-done((f32[256,256]{1,0:T(8,128)S(1)}, f32[256,256]{1,0:T(8,128)S(1)}, u32[]{:S(2)}, u32[]{:S(2)}) %collective-permute-start) | collective-permute-done | bytes 262176 | tf_op jit(solution)/shard_map/while/body/eval_jaxpr/ppermute | solution.py:20
  613.6 7.0 %collective-permute-done = f32[256,256]{1,0:T(8,128)S(1)} collective-permute-done((f32[256,256]{1,0:T(8,128)S(1)}, f32[256,256]{1,0:T(8,128)S(1)}, u32[]{:S(2)}, u32[]{:S(2)}) %collective-permute-start) | collective-permute-done | bytes 262176 | tf_op jit(solution)/shard_map/while/body/eval_jaxpr/ppermute | solution.py:20
  (238 shorter events, 105.7 us)
Async XLA Ops:
  2.2 26.9 %collective-permute-start.1 = (f32[4,256,256]{1,2,0:T(8,128)S(1)}, f32[4,256,256]{1,2,0:T(8,128)}, u32[]{:S(2)}, u32[]{:S(2)}) collective-permute-start(f32[4,256,256]{1,2,0:T(8,128)S(1)} %bitcast.392), channel_id=1, source_target_pairs={{0,1},{1,0},{2,3},{3,2},{4,5},{5,4},{6,7},{7,6},{8,9},{9,8},{10,11... | collective-permute-start | bytes 3145736 | tf_op jit(solution)/shard_map/ppermute | solution.py:14
  81.2 0.8 copy-start.8
  86.8 27.6 %collective-permute-start.2 = (f32[4,256,256]{1,2,0:T(8,128)S(1)}, f32[4,256,256]{1,2,0:T(8,128)}, u32[]{:S(2)}, u32[]{:S(2)}) collective-permute-start(f32[4,256,256]{1,2,0:T(8,128)S(1)} %pad_maximum_fusion), channel_id=1, source_target_pairs={{0,2},{2,0},{1,3},{3,1},{4,6},{6,4},{5,7},{7,5},{8,10},{10,8},{9,1... | collective-permute-start | bytes 3145736 | tf_op jit(solution)/shard_map/ppermute | solution.py:14
  166.3 0.8 copy-start.9
  171.8 25.8 %collective-permute-start.3 = (f32[4,256,256]{1,2,0:T(8,128)S(1)}, f32[4,256,256]{1,2,0:T(8,128)}, u32[]{:S(2)}, u32[]{:S(2)}) collective-permute-start(f32[4,256,256]{1,2,0:T(8,128)S(1)} %pad_maximum_fusion.1), channel_id=1, source_target_pairs={{0,4},{4,0},{1,5},{5,1},{2,6},{6,2},{3,7},{7,3},{8,12},{12,8},{9,1... | collective-permute-start | bytes 3145736 | tf_op jit(solution)/shard_map/ppermute | solution.py:14
  249.6 0.8 copy-start.10
  255.1 49.6 %collective-permute-start.4 = (f32[4,256,256]{1,2,0:T(8,128)S(1)}, f32[4,256,256]{1,2,0:T(8,128)}, u32[]{:S(2)}, u32[]{:S(2)}) collective-permute-start(f32[4,256,256]{1,2,0:T(8,128)S(1)} %pad_maximum_fusion.2), channel_id=1, source_target_pairs={{0,8},{8,0},{1,9},{9,1},{2,10},{10,2},{3,11},{11,3},{4,12},{12,4},... | collective-permute-start | bytes 3145736 | tf_op jit(solution)/shard_map/ppermute | solution.py:14
  356.8 0.8 copy-start.11
  360.1 2.2 copy-start.2
  360.7 1.6 copy-start.4
  362.3 8.7 %copy-start.1 = (f32[1,256,256]{2,1,0:T(8,128)S(1)}, f32[1,256,256]{2,1,0:T(8,128)}, u32[]{:S(2)}) copy-start(f32[1,256,256]{2,1,0:T(8,128)} %param.10) | copy-start | bytes 786436
  362.4 53.8 %collective-permute-start.5 = (f32[4,256,256]{1,2,0:T(8,128)S(1)}, f32[4,256,256]{1,2,0:T(8,128)}, u32[]{:S(2)}, u32[]{:S(2)}) collective-permute-start(f32[4,256,256]{1,2,0:T(8,128)S(1)} %pad_maximum_fusion.3), channel_id=1, source_target_pairs={{0,16},{16,0},{1,17},{17,1},{2,18},{18,2},{3,19},{19,3},{4,20},{20... | collective-permute-start | bytes 3145736 | tf_op jit(solution)/shard_map/ppermute | solution.py:14
  371.1 45.1 %copy-start.3 = (f32[1,256,256]{1,2,0:T(8,128)S(1)}, f32[1,256,256]{1,2,0:T(8,128)}, u32[]{:S(2)}) copy-start(f32[1,256,256]{1,2,0:T(8,128)} %copy-done.2) | copy-start | bytes 786436
  371.1 45.1 %copy-start.5 = (f32[1,256,256]{1,2,0:T(8,128)S(1)}, f32[1,256,256]{1,2,0:T(8,128)}, u32[]{:S(2)}) copy-start(f32[1,256,256]{1,2,0:T(8,128)} %copy-done.4) | copy-start | bytes 786436
  443.8 0.8 copy-start.12
  446.1 1.6 copy-start.6
  447.9 27.7 %copy-start.7 = (f32[128,512]{0,1:T(8,128)S(1)}, f32[128,512]{0,1:T(8,128)}, u32[]{:S(2)}) copy-start(f32[128,512]{0,1:T(8,128)} %fusion.83) | copy-start | bytes 786436
  480.4 8.9 %collective-permute-start = (f32[256,256]{1,0:T(8,128)S(1)}, f32[256,256]{1,0:T(8,128)S(1)}, u32[]{:S(2)}, u32[]{:S(2)}) collective-permute-start(f32[256,256]{1,0:T(8,128)S(1)} %fusion.306), channel_id=1, source_target_pairs={{0,32},{32,64},{64,96},{96,128},{128,160},{160,192},{192,224},{224... | collective-permute-start | bytes 786440 | tf_op jit(solution)/shard_map/while/body/eval_jaxpr/ppermute | solution.py:20
  489.8 8.9 %collective-permute-start = (f32[256,256]{1,0:T(8,128)S(1)}, f32[256,256]{1,0:T(8,128)S(1)}, u32[]{:S(2)}, u32[]{:S(2)}) collective-permute-start(f32[256,256]{1,0:T(8,128)S(1)} %fusion.306), channel_id=1, source_target_pairs={{0,32},{32,64},{64,96},{96,128},{128,160},{160,192},{192,224},{224... | collective-permute-start | bytes 786440 | tf_op jit(solution)/shard_map/while/body/eval_jaxpr/ppermute | solution.py:20
  499.2 8.9 %collective-permute-start = (f32[256,256]{1,0:T(8,128)S(1)}, f32[256,256]{1,0:T(8,128)S(1)}, u32[]{:S(2)}, u32[]{:S(2)}) collective-permute-start(f32[256,256]{1,0:T(8,128)S(1)} %fusion.306), channel_id=1, source_target_pairs={{0,32},{32,64},{64,96},{96,128},{128,160},{160,192},{192,224},{224... | collective-permute-start | bytes 786440 | tf_op jit(solution)/shard_map/while/body/eval_jaxpr/ppermute | solution.py:20
  508.5 8.9 %collective-permute-start = (f32[256,256]{1,0:T(8,128)S(1)}, f32[256,256]{1,0:T(8,128)S(1)}, u32[]{:S(2)}, u32[]{:S(2)}) collective-permute-start(f32[256,256]{1,0:T(8,128)S(1)} %fusion.306), channel_id=1, source_target_pairs={{0,32},{32,64},{64,96},{96,128},{128,160},{160,192},{192,224},{224... | collective-permute-start | bytes 786440 | tf_op jit(solution)/shard_map/while/body/eval_jaxpr/ppermute | solution.py:20
  517.9 8.9 %collective-permute-start = (f32[256,256]{1,0:T(8,128)S(1)}, f32[256,256]{1,0:T(8,128)S(1)}, u32[]{:S(2)}, u32[]{:S(2)}) collective-permute-start(f32[256,256]{1,0:T(8,128)S(1)} %fusion.306), channel_id=1, source_target_pairs={{0,32},{32,64},{64,96},{96,128},{128,160},{160,192},{192,224},{224... | collective-permute-start | bytes 786440 | tf_op jit(solution)/shard_map/while/body/eval_jaxpr/ppermute | solution.py:20
  527.3 8.9 %collective-permute-start = (f32[256,256]{1,0:T(8,128)S(1)}, f32[256,256]{1,0:T(8,128)S(1)}, u32[]{:S(2)}, u32[]{:S(2)}) collective-permute-start(f32[256,256]{1,0:T(8,128)S(1)} %fusion.306), channel_id=1, source_target_pairs={{0,32},{32,64},{64,96},{96,128},{128,160},{160,192},{192,224},{224... | collective-permute-start | bytes 786440 | tf_op jit(solution)/shard_map/while/body/eval_jaxpr/ppermute | solution.py:20
  536.7 8.9 %collective-permute-start = (f32[256,256]{1,0:T(8,128)S(1)}, f32[256,256]{1,0:T(8,128)S(1)}, u32[]{:S(2)}, u32[]{:S(2)}) collective-permute-start(f32[256,256]{1,0:T(8,128)S(1)} %fusion.306), channel_id=1, source_target_pairs={{0,32},{32,64},{64,96},{96,128},{128,160},{160,192},{192,224},{224... | collective-permute-start | bytes 786440 | tf_op jit(solution)/shard_map/while/body/eval_jaxpr/ppermute | solution.py:20
  546.0 8.9 %collective-permute-start = (f32[256,256]{1,0:T(8,128)S(1)}, f32[256,256]{1,0:T(8,128)S(1)}, u32[]{:S(2)}, u32[]{:S(2)}) collective-permute-start(f32[256,256]{1,0:T(8,128)S(1)} %fusion.306), channel_id=1, source_target_pairs={{0,32},{32,64},{64,96},{96,128},{128,160},{160,192},{192,224},{224... | collective-permute-start | bytes 786440 | tf_op jit(solution)/shard_map/while/body/eval_jaxpr/ppermute | solution.py:20
  555.4 8.9 %collective-permute-start = (f32[256,256]{1,0:T(8,128)S(1)}, f32[256,256]{1,0:T(8,128)S(1)}, u32[]{:S(2)}, u32[]{:S(2)}) collective-permute-start(f32[256,256]{1,0:T(8,128)S(1)} %fusion.306), channel_id=1, source_target_pairs={{0,32},{32,64},{64,96},{96,128},{128,160},{160,192},{192,224},{224... | collective-permute-start | bytes 786440 | tf_op jit(solution)/shard_map/while/body/eval_jaxpr/ppermute | solution.py:20
  564.8 8.9 %collective-permute-start = (f32[256,256]{1,0:T(8,128)S(1)}, f32[256,256]{1,0:T(8,128)S(1)}, u32[]{:S(2)}, u32[]{:S(2)}) collective-permute-start(f32[256,256]{1,0:T(8,128)S(1)} %fusion.306), channel_id=1, source_target_pairs={{0,32},{32,64},{64,96},{96,128},{128,160},{160,192},{192,224},{224... | collective-permute-start | bytes 786440 | tf_op jit(solution)/shard_map/while/body/eval_jaxpr/ppermute | solution.py:20
  574.1 8.9 %collective-permute-start = (f32[256,256]{1,0:T(8,128)S(1)}, f32[256,256]{1,0:T(8,128)S(1)}, u32[]{:S(2)}, u32[]{:S(2)}) collective-permute-start(f32[256,256]{1,0:T(8,128)S(1)} %fusion.306), channel_id=1, source_target_pairs={{0,32},{32,64},{64,96},{96,128},{128,160},{160,192},{192,224},{224... | collective-permute-start | bytes 786440 | tf_op jit(solution)/shard_map/while/body/eval_jaxpr/ppermute | solution.py:20
  583.5 8.9 %collective-permute-start = (f32[256,256]{1,0:T(8,128)S(1)}, f32[256,256]{1,0:T(8,128)S(1)}, u32[]{:S(2)}, u32[]{:S(2)}) collective-permute-start(f32[256,256]{1,0:T(8,128)S(1)} %fusion.306), channel_id=1, source_target_pairs={{0,32},{32,64},{64,96},{96,128},{128,160},{160,192},{192,224},{224... | collective-permute-start | bytes 786440 | tf_op jit(solution)/shard_map/while/body/eval_jaxpr/ppermute | solution.py:20
  592.9 8.9 %collective-permute-start = (f32[256,256]{1,0:T(8,128)S(1)}, f32[256,256]{1,0:T(8,128)S(1)}, u32[]{:S(2)}, u32[]{:S(2)}) collective-permute-start(f32[256,256]{1,0:T(8,128)S(1)} %fusion.306), channel_id=1, source_target_pairs={{0,32},{32,64},{64,96},{96,128},{128,160},{160,192},{192,224},{224... | collective-permute-start | bytes 786440 | tf_op jit(solution)/shard_map/while/body/eval_jaxpr/ppermute | solution.py:20
  602.3 8.9 %collective-permute-start = (f32[256,256]{1,0:T(8,128)S(1)}, f32[256,256]{1,0:T(8,128)S(1)}, u32[]{:S(2)}, u32[]{:S(2)}) collective-permute-start(f32[256,256]{1,0:T(8,128)S(1)} %fusion.306), channel_id=1, source_target_pairs={{0,32},{32,64},{64,96},{96,128},{128,160},{160,192},{192,224},{224... | collective-permute-start | bytes 786440 | tf_op jit(solution)/shard_map/while/body/eval_jaxpr/ppermute | solution.py:20
  611.6 8.9 %collective-permute-start = (f32[256,256]{1,0:T(8,128)S(1)}, f32[256,256]{1,0:T(8,128)S(1)}, u32[]{:S(2)}, u32[]{:S(2)}) collective-permute-start(f32[256,256]{1,0:T(8,128)S(1)} %fusion.306), channel_id=1, source_target_pairs={{0,32},{32,64},{64,96},{96,128},{128,160},{160,192},{192,224},{224... | collective-permute-start | bytes 786440 | tf_op jit(solution)/shard_map/while/body/eval_jaxpr/ppermute | solution.py:20
  620.6 1.1 copy-start
where the time goes:
time: 632 us; the launch traced here: 622 us
  waiting for transfers between devices  262 us (41%)
  other arithmetic  246 us (39%)
  starting transfers between devices  55.1 us (9%)
  matrix products  49.7 us (8%)
  local copies, waits for them, and re-layouts  6.56 us (1%)
    ppermute x5, waiting for transfers between devices, partner(): return lax.ppermute(block, axis, route)  157 us
    another operation x30, other arithmetic, block_solve(): factor = jnp.linalg.cholesky(normal_matrix)  127 us
    another operation x20, other arithmetic, block_solve(): jax.scipy.linalg.cho_solve((factor, True), transpose_times(system, right))  109 us
    ppermute x15, waiting for transfers between devices, from_behind(): return lax.ppermute(block, axis, route)  105 us
    ppermute x15, starting transfers between devices, from_behind(): return lax.ppermute(block, axis, route)  28.8 us
    dot_general x52, matrix products, matmul(): jnp.dot(left, right, precision=lax.Precision.HIGHEST, preferred_element_t...  27.3 us
    ppermute x5, starting transfers between devices, partner(): return lax.ppermute(block, axis, route)  26.2 us
  transfers between devices with their start and end apart: 20, of which 20 were waited for; matrix products, arithmetic and copies ran while one was open for 0% of the time, Pallas kernels for 0%

commit v1 on v0

v1 whole, which is shorter than its diff:
```python
import functools

import jax
import jax.numpy as jnp
from jax import lax
from jax.experimental import pallas as pl
from jax.experimental.pallas import tpu as pltpu
from jax.sharding import PartitionSpec as P

F32 = jnp.float32
BF16 = jnp.bfloat16
MESH = pl.DeviceIdType.MESH
DOUBLINGS = 16
CHUNKS = 8
LEVELS = 5
OWN = 8 * LEVELS
PARTNER = OWN + 4
BLOCKS = OWN + 5
FINAL_R = 8 * (LEVELS - 1) + 6
FINAL_T = FINAL_R + 1


def split(value):
    high = value.astype(BF16)
    return high, (value - high.astype(F32)).astype(BF16)


def dot(left, right):
    return jnp.dot(left, right, preferred_element_type=F32)


def split_dot(left, right):
    return dot(left[0], right[0]) + (dot(left[0], right[1]) + dot(left[1], right[0]))


def matmul(left, right):
    return split_dot(split(left), split(right))


def kernel(
    slabs, incident, down, bounced,
    buf, power, inverse, coupled, field, arrive, leave, handed, handing, extra, pair_t, own_t,
    load_sem, store_sem, tree_send, tree_recv, cast_send, cast_recv,
    chain_send, chain_recv, hand_send, hand_recv, extra_send, extra_recv, part_send, part_recv,
):
    slab = lax.axis_index("slab")
    depth = lax.axis_index("depth")
    x = lax.rem(slab, 4)
    z = lax.div(slab, 4)
    core = lax.rem(depth, 2)
    y = lax.div(depth, 2)
    chips = lax.axis_size("depth") // 2
    order = buf.shape[1]
    rows = field.shape[0] // CHUNKS
    band = order // CHUNKS

    loads = [
        pltpu.make_async_copy(slabs.at[0, 0, i], buf.at[OWN + i], load_sem.at[i]) for i in range(4)
    ]
    loads.append(pltpu.make_async_copy(incident.at[0], field, load_sem.at[4]))
    for load in loads:
        load.start()

    def at(px, pz):
        return lax.rem(pz + 16, 8) * 4 + lax.rem(px + 8, 4)

    rt_x = 1 - core
    qu_x = 2 + core
    root_z = 3

    barrier = pltpu.get_barrier_semaphore()

    def greet(**target):
        pl.semaphore_signal(barrier, inc=1, device_id=target, device_id_type=MESH)

    for px, pz in ((1, 0), (-1, 0), (2, 0), (0, 1), (0, -1), (0, 2), (0, -2), (1, 1), (-1, -1), (1, -1), (-1, 1)):
        greet(slab=at(x + px, z + pz))
    greet(depth=depth + 1 - 2 * core)

    @pl.when(y > 0)
    def _():
        greet(depth=depth - 2)

    @pl.when(y < chips - 1)
    def _():
        greet(depth=depth + 2)

    pl.semaphore_wait(barrier, 12 + (y > 0).astype(jnp.int32) + (y < chips - 1).astype(jnp.int32))

    def slot(level, pair, part):
        return level * 8 + pair * 2 + part

    outer = (x == 0) | (x == 3)
    on_rt = x == rt_x
    on_qu = x == qu_x
    z2 = lax.rem(z, 2)
    z4 = lax.rem(z, 4)
    mirror = at(3 - x, z)
    crossing2 = (on_qu & (z2 == 0)) | (on_rt & (z2 == 1))
    merged2 = (on_rt & (z2 == 0)) | (on_qu & (z2 == 1))
    inner3 = (on_qu & (z4 == 1)) | (on_rt & (z4 == 2))
    ahead3 = jnp.where(z4 < 2, 1, -1)
    root = on_rt & (z == root_z)
    source4 = (on_rt & ((z == 1) | (z == 5))) | (on_qu & (z == 2))
    true = x >= 0
    false = x < 0
    routes = [
        [(true, at(x + 1 - 2 * lax.rem(x, 2), z), 2)],
        [
            (jnp.logical_not(outer), jnp.where(core == 0, mirror, at(x + 2, z)), 2),
            (outer == (core == 0), at(x + 1 - 2 * lax.rem(x, 2), z), core),
        ],
        [
            (crossing2, mirror, 1),
            (crossing2, at(x, z + 1 - 2 * z2), 2),
        ],
        [
            (inner3, mirror, 1),
            (merged2, at(x, z + ahead3), jnp.where(inner3, 2, 0)),
        ],
        [
            (source4, at(rt_x, root_z), jnp.where(on_qu, 1, jnp.where(z == 1, 0, 2))),
        ],
    ]
    computes = [
        true,
        on_rt | on_qu,
        merged2,
        (on_rt & (z4 == 1)) | (on_qu & (z4 == 2)),
        root,
    ]
    local = [3, 1 - core, 0, 3, 3]

    def tree_copy(level, number, part, source):
        sends, target, pair = routes[level][number]
        return sends, pltpu.make_async_remote_copy(
            src_ref=buf.at[source],
            dst_ref=buf.at[slot(level, pair, part)],
            send_sem=tree_send.at[level, number, part],
            recv_sem=tree_recv.at[level, pair, part],
            device_id={"slab": target},
            device_id_type=MESH,
        )

    def send_part(level, part, source):
        for number in range(len(routes[level])):
            sends, copy = tree_copy(level, number, part, source)

            @pl.when(sends)
            def _():
                copy.start()

    def await_part(level, pair, part):
        pltpu.make_async_remote_copy(
            src_ref=buf.at[slot(level, pair, part)],
            dst_ref=buf.at[slot(level, pair, part)],
            send_sem=tree_send.at[level, 0, part],
            recv_sem=tree_recv.at[level, pair, part],
            device_id={"slab": slab},
            device_id_type=MESH,
        ).wait_recv()

    for load in loads[:4]:
        load.wait()
    odd = lax.rem(x, 2) == 1
    first_pair = jnp.where(odd, OWN, OWN + 2)
    add_pair = jnp.where(odd, OWN + 2, OWN)
    send_part(0, 0, first_pair)
    send_part(0, 1, first_pair + 1)

    def operand(level, pair, part):
        if level == 0:
            if pair == 2:
                return slot(0, 2, part)
            return (add_pair if pair == 0 else first_pair) + part
        own = slot(level - 1, 3, part)
        known = local[level]
        if isinstance(known, int):
            return own if known == pair else slot(level, pair, part)
        return jnp.where(known == pair, own, slot(level, pair, part))

    def arrived(level, pair, part):
        if level == 0:
            if pair == 2:
                await_part(0, 2, part)
            return
        known = local[level]
        if isinstance(known, int):
            if known != pair:
                await_part(level, pair, part)
            return

        @pl.when(known != pair)
        def _():
            await_part(level, pair, part)

    def merge(level):
        arrived(level, 1, 0)
        arrived(level, 2, 0)
        near = buf[operand(level, 1, 0)]
        far = split(buf[operand(level, 2, 0)])
        system = split_dot(split(near), far)
        ones = lax.broadcasted_iota(jnp.int32, (order, order), 0) == lax.broadcasted_iota(jnp.int32, (order, order), 1)
        inverse[...] = system + jnp.where(ones, 1.0, 0.0)
        power[...] = system

        def double(_, carry):
            halves = split(power[...])
            squared = split_dot(halves, halves)
            power[...] = squared
            whole = inverse[...]
            inverse[...] = whole + split_dot(split(squared), split(whole))
            return carry

        lax.fori_loop(0, DOUBLINGS - 1, double, 0)
        solved = split(inverse[...])
        coupled[...] = split_dot(far, solved)
        arrived(level, 0, 1)
        right = split(buf[operand(level, 0, 1)])
        through = split_dot(solved, right)
        turned = split_dot(split(coupled[...]), right)
        arrived(level, 1, 1)
        arrived(level, 0, 0)
        buf[slot(level, 3, 0)] = buf[operand(level, 0, 0)] + matmul(buf[operand(level, 1, 1)], turned)
        if level + 1 < LEVELS:
            send_part(level + 1, 0, slot(level, 3, 0))
        arrived(level, 2, 1)
        buf[slot(level, 3, 1)] = matmul(buf[operand(level, 2, 1)], through)
        if level + 1 < LEVELS:
            send_part(level + 1, 1, slot(level, 3, 1))

    for level in range(LEVELS):

        @pl.when(computes[level])
        def _(level=level):
            merge(level)

    dx = lax.rem(x - rt_x + 4, 4)
    dz = lax.rem(z - root_z + 8, 8)
    x_first = core == 0
    x_line = jnp.logical_not(x_first) | (dz == 0)
    z_line = x_first | (dx == 0)
    children = [
        (x_line & (dx <= 1), at(x + 1, z)),
        (x_line & (dx == 0), at(x - 1, z)),
        (z_line & (dz <= 3), at(x, z + 1)),
        (z_line & ((dz == 0) | (dz >= 6)), at(x, z - 1)),
    ]

    def cast_copy(which, chunk, child):
        place = buf.at[FINAL_R + which, pl.ds(chunk * band, band)]
        return pltpu.make_async_remote_copy(
            src_ref=place,
            dst_ref=place,
            send_sem=cast_send.at[which, chunk, child],
            recv_sem=cast_recv.at[which, chunk],
            device_id={"slab": children[child][1]},
            device_id_type=MESH,
        )

    def part_copy(chunk):
        return pltpu.make_async_remote_copy(
            src_ref=buf.at[FINAL_T, pl.ds(chunk * band, band)],
            dst_ref=buf.at[PARTNER, pl.ds(chunk * band, band)],
            send_sem=part_send.at[chunk],
            recv_sem=part_recv.at[chunk],
            device_id={"depth": depth + 1 - 2 * core},
            device_id_type=MESH,
        )

    def forward(which):
        for chunk in range(CHUNKS):

            @pl.when(jnp.logical_not(root))
            def _():
                cast_copy(which, chunk, 0).wait_recv()

            for child in range(4):

                @pl.when(children[child][0])
                def _():
                    cast_copy(which, chunk, child).start()

            if which == 1:

                @pl.when(core == 1)
                def _():
                    part_copy(chunk).start()

    forward(1)
    loads[4].wait()

    @pl.when((y > 0) | (core == 1))
    def _():
        forward(0)

    extra_copy = pltpu.make_async_remote_copy(
        src_ref=extra,
        dst_ref=extra,
        send_sem=extra_send,
        recv_sem=extra_recv,
        device_id={"depth": depth + 1 - 2 * core},
        device_id_type=MESH,
    )

    def keep_split(ref, value):
        ref[0], ref[1] = split(value)

    def chain_copy(chunk):
        return pltpu.make_async_remote_copy(
            src_ref=leave.at[pl.ds(chunk * rows, rows)],
            dst_ref=arrive.at[pl.ds(chunk * rows, rows)],
            send_sem=chain_send.at[chunk],
            recv_sem=chain_recv.at[chunk],
            device_id={"depth": lax.rem(depth + 2, 2 * chips)},
            device_id_type=MESH,
        )

    def hand_copy(chunk):
        return pltpu.make_async_remote_copy(
            src_ref=handing.at[pl.ds(chunk * rows, rows)],
            dst_ref=handed.at[pl.ds(chunk * rows, rows)],
            send_sem=hand_send.at[chunk],
            recv_sem=hand_recv.at[chunk],
            device_id={"depth": depth + 1 - 2 * core},
            device_id_type=MESH,
        )

    @pl.when(core == 1)
    def _():
        keep_split(own_t, buf[FINAL_T].T)
        extra[...] = split_dot(split(field[...]), (own_t[0], own_t[1]))
        extra_copy.start()
        for chunk in range(CHUNKS):
            part = pl.ds(chunk * rows, rows)
            hand_copy(chunk).wait_recv()
            field[part] += handed[part]

    @pl.when(core == 0)
    def _():
        keep_split(own_t, buf[FINAL_T].T)
        for chunk in range(CHUNKS):
            part_copy(chunk).wait_recv()
        keep_split(pair_t, matmul(buf[PARTNER], buf[FINAL_T]).T)
        extra_copy.wait_recv()
        for chunk in range(CHUNKS):
            part = pl.ds(chunk * rows, rows)

            @pl.when(y > 0)
            def _():
                chain_copy(chunk).wait_recv()
                field[part] += arrive[part]

            halves = split(field[part])

            @pl.when(y < chips - 1)
            def _():
                leave[part] = split_dot(halves, (pair_t[0], pair_t[1])) + extra[part]
                chain_copy(chunk).start()

            handing[part] = split_dot(halves, (own_t[0], own_t[1]))
            hand_copy(chunk).start()

    store_down = pltpu.make_async_copy(field, down.at[0], store_sem.at[0])
    store_down.start()

    @pl.when((y == 0) & (core == 0))
    def _():
        forward(0)

    arrive[...] = matmul(field[...], buf[FINAL_R].T)
    store_bounced = pltpu.make_async_copy(arrive, bounced.at[0], store_sem.at[1])
    store_bounced.start()

    for level in range(LEVELS):
        for number in range(len(routes[level])):
            for part in range(2):
                sends, copy = tree_copy(level, number, part, OWN)

                @pl.when(sends)
                def _():
                    copy.wait_send()

    for which in range(2):
        for chunk in range(CHUNKS):
            for child in range(4):

                @pl.when(children[child][0])
                def _():
                    cast_copy(which, chunk, child).wait_send()

    @pl.when(core == 1)
    def _():
        extra_copy.wait_send()
        for chunk in range(CHUNKS):
            part_copy(chunk).wait_send()

    @pl.when(core == 0)
    def _():
        for chunk in range(CHUNKS):
            hand_copy(chunk).wait_send()

        @pl.when(y < chips - 1)
        def _():
            for chunk in range(CHUNKS):
                chain_copy(chunk).wait_send()

    store_down.wait()
    store_bounced.wait()


def shards(slabs, incident):
    order = slabs.shape[-1]
    rows = incident.shape[1]
    block = jax.ShapeDtypeStruct(incident.shape, F32)
    matrix = pltpu.VMEM((order, order), F32)
    halves = pltpu.VMEM((2, order, order), BF16)
    fields = pltpu.VMEM((rows, order), F32)
    dma = pltpu.SemaphoreType.DMA
    return pl.pallas_call(
        kernel,
        out_shape=(block, block),
        in_specs=[pl.BlockSpec(memory_space=pl.ANY)] * 2,
        out_specs=[pl.BlockSpec(memory_space=pl.ANY)] * 2,
        scratch_shapes=[
            pltpu.VMEM((BLOCKS, order, order), F32),
            matrix, matrix, matrix,
            fields, fields, fields, fields, fields, fields,
            halves, halves,
            dma((5,)), dma((2,)),
            dma((LEVELS, 2, 2)), dma((LEVELS, 3, 2)),
            dma((2, CHUNKS, 4)), dma((2, CHUNKS)),
            dma((CHUNKS,)), dma((CHUNKS,)),
            dma((CHUNKS,)), dma((CHUNKS,)),
            dma, dma,
            dma((CHUNKS,)), dma((CHUNKS,)),
        ],
        compiler_params=pltpu.CompilerParams(collective_id=0, has_side_effects=True, vmem_limit_bytes=60 * 2**20),
        name="layers",
    )(slabs, incident)


def solution(mesh):
    placed = (P("depth", "slab", None, None, None), P("depth", "slab", None))
    return jax.shard_map(
        shards,
        mesh=mesh,
        in_specs=placed,
        out_specs=(P("depth", "slab", None), P("depth", "slab", None)),
        check_vma=False,
    )
```

time: 632 us -> 147 us (0.23)
  the two profiles are of different devices: /device:TPU:34 before, /device:TPU:63 now
where the time goes in v1:
time: 147 us
  Pallas kernels  144 us (98%)
  local copies, waits for them, and re-layouts  2.42 us (2%)
    pallas_call x1, Pallas kernels, shards(): pl.pallas_call(kernel, out_shape=(block, block), in_specs=[pl.BlockSpec(m...  144 us

profile of v1, /device:TPU:63, one launch (start us, length us, event | category | flops | bytes accessed | tf_op | source)
XLA Modules:
  0.0 146.6 jit_solution(15813924241656811732)
XLA Ops:
  0.6 143.6 %layers.1 = (f32[1,256,256]{2,1,0:T(8,128)}, f32[1,256,256]{2,1,0:T(8,128)}) custom-call(f32[1,1,4,256,256]{4,3,2,1,0:T(8,128)} %slabs.1, f32[1,256,256]{2,1,0:T(8,128)} %incident.1), custom_call_target="tpu_custom_call" | custom-call | tf_op jit(solution)/shard_map/layers/pallas_call | solution.py:420
  144.2 0.0 copy-start
  144.2 1.7 %copy.6 = f32[1,256,256]{2,1,0:T(8,128)} copy(f32[1,256,256]{2,1,0:T(8,128)} %get-tuple-element.4) | data formatting | bytes 524288
  145.9 0.0 copy-done
  145.9 0.7 copy.7
Async XLA Ops:
  144.2 1.7 %copy-start = (f32[1,256,256]{2,1,0:T(8,128)S(1)}, f32[1,256,256]{2,1,0:T(8,128)}, u32[]{:S(2)}) copy-start(f32[1,256,256]{2,1,0:T(8,128)} %get-tuple-element.5) | copy-start | bytes 786436

commit v2 on v1

--- a/solution.py
+++ b/solution.py
@@ -10,8 +10,13 @@
 F32 = jnp.float32
 BF16 = jnp.bfloat16
 MESH = pl.DeviceIdType.MESH
-DOUBLINGS = 16
+DOUBLINGS = 3
+MORE_DOUBLINGS = 24
+REMAINDER = 1e-6
 CHUNKS = 8
+CASTS = 8
+ROOT_Z = 1
+EARLY = 2
 LEVELS = 5
 OWN = 8 * LEVELS
 PARTNER = OWN + 4
@@ -38,10 +43,11 @@
 
 
 def kernel(
-    slabs, incident, down, bounced,
-    buf, power, inverse, coupled, field, arrive, leave, handed, handing, extra, pair_t, own_t,
+    doublings, slabs, incident, down, bounced, settled,
+    buf, power, inverse, coupled, field, arrive, leave, handed, handing, extra, pair_t, bounce_t,
     load_sem, store_sem, tree_send, tree_recv, cast_send, cast_recv,
     chain_send, chain_recv, hand_send, hand_recv, extra_send, extra_recv, part_send, part_recv,
+    heads, mark, head_send, head_recv,
 ):
     slab = lax.axis_index("slab")
     depth = lax.axis_index("depth")
@@ -52,7 +58,7 @@
     chips = lax.axis_size("depth") // 2
     order = buf.shape[1]
     rows = field.shape[0] // CHUNKS
-    band = order // CHUNKS
+    band = order // CASTS
 
     loads = [
         pltpu.make_async_copy(slabs.at[0, 0, i], buf.at[OWN + i], load_sem.at[i]) for i in range(4)
@@ -66,26 +72,7 @@
 
     rt_x = 1 - core
     qu_x = 2 + core
-    root_z = 3
-
-    barrier = pltpu.get_barrier_semaphore()
-
-    def greet(**target):
-        pl.semaphore_signal(barrier, inc=1, device_id=target, device_id_type=MESH)
-
-    for px, pz in ((1, 0), (-1, 0), (2, 0), (0, 1), (0, -1), (0, 2), (0, -2), (1, 1), (-1, -1), (1, -1), (-1, 1)):
-        greet(slab=at(x + px, z + pz))
-    greet(depth=depth + 1 - 2 * core)
-
-    @pl.when(y > 0)
-    def _():
-        greet(depth=depth - 2)
-
-    @pl.when(y < chips - 1)
-    def _():
-        greet(depth=depth + 2)
-
-    pl.semaphore_wait(barrier, 12 + (y > 0).astype(jnp.int32) + (y < chips - 1).astype(jnp.int32))
+    root_z = ROOT_Z
 
     def slot(level, pair, part):
         return level * 8 + pair * 2 + part
@@ -101,7 +88,34 @@
     inner3 = (on_qu & (z4 == 1)) | (on_rt & (z4 == 2))
     ahead3 = jnp.where(z4 < 2, 1, -1)
     root = on_rt & (z == root_z)
-    source4 = (on_rt & ((z == 1) | (z == 5))) | (on_qu & (z == 2))
+    rt_rows = [row for row in (1, 5) if row != root_z]
+    sources = [(rt_x, row) for row in rt_rows] + [(qu_x, 2)]
+    source4 = on_qu & (z == 2)
+    for row in rt_rows:
+        source4 = source4 | (on_rt & (z == row))
+
+    barrier = pltpu.get_barrier_semaphore()
+
+    def greet(**target):
+        pl.semaphore_signal(barrier, inc=1, device_id=target, device_id_type=MESH)
+
+    for px, pz in ((1, 0), (-1, 0), (2, 0), (0, 1), (0, -1)):
+        greet(slab=at(x + px, z + pz))
+    for step in range(1, 2 * chips):
+        greet(depth=lax.rem(depth + step, 2 * chips))
+
+    @pl.when(source4)
+    def _():
+        greet(slab=at(rt_x, root_z))
+
+    @pl.when(root)
+    def _():
+        for px, pz in sources:
+            greet(slab=at(px, pz))
+
+    met = [source4] + [root] * len(sources)
+    pl.semaphore_wait(barrier, 4 + 2 * chips + sum(flag.astype(jnp.int32) for flag in met))
+
     true = x >= 0
     false = x < 0
     routes = [
@@ -129,7 +143,7 @@
         (on_rt & (z4 == 1)) | (on_qu & (z4 == 2)),
         root,
     ]
-    local = [3, 1 - core, 0, 3, 3]
+    local = [3, 1 - core, 0, 3, {1: 0, 5: 2}.get(ROOT_Z, 3)]
 
     def tree_copy(level, number, part, source):
         sends, target, pair = routes[level][number]
@@ -204,15 +218,24 @@
         inverse[...] = system + jnp.where(ones, 1.0, 0.0)
         power[...] = system
 
-        def double(_, carry):
-            halves = split(power[...])
+        def double(halves):
             squared = split_dot(halves, halves)
             power[...] = squared
             whole = inverse[...]
             inverse[...] = whole + split_dot(split(squared), split(whole))
-            return carry
-
-        lax.fori_loop(0, DOUBLINGS - 1, double, 0)
+
+        if doublings <= DOUBLINGS:
+            for _ in range(doublings - 1):
+                double(split(power[...]))
+            left = jnp.sum(jnp.square(power[...]), axis=(0, 1), keepdims=True)
+            inverse[...] += jnp.where(left < REMAINDER, 0.0, jnp.nan)
+        else:
+
+            def step(_, carry):
+                double(split(power[...]))
+                return carry
+
+            lax.fori_loop(0, doublings - 1, step, 0)
         solved = split(inverse[...])
         coupled[...] = split_dot(far, solved)
         arrived(level, 0, 1)
@@ -241,8 +264,8 @@
     x_line = jnp.logical_not(x_first) | (dz == 0)
     z_line = x_first | (dx == 0)
     children = [
-        (x_line & (dx <= 1), at(x + 1, z)),
-        (x_line & (dx == 0), at(x - 1, z)),
+        (x_line & ((dx == 0) | (x_first & (dx == 1))), at(x + 1, z)),
+        (x_line & ((dx == 0) | (jnp.logical_not(x_first) & (dx == 3))), at(x - 1, z)),
         (z_line & (dz <= 3), at(x, z + 1)),
         (z_line & ((dz == 0) | (dz >= 6)), at(x, z - 1)),
     ]
@@ -268,8 +291,18 @@
             device_id_type=MESH,
         )
 
+    def head_copy(step):
+        return pltpu.make_async_remote_copy(
+            src_ref=buf.at[FINAL_T, pl.ds(0, 8), pl.ds(0, 128)],
+            dst_ref=heads.at[step],
+            send_sem=head_send.at[step],
+            recv_sem=head_recv.at[step],
+            device_id={"depth": lax.rem(depth + step, 2 * chips)},
+            device_id_type=MESH,
+        )
+
     def forward(which):
-        for chunk in range(CHUNKS):
+        for chunk in range(CASTS):
 
             @pl.when(jnp.logical_not(root))
             def _():
@@ -282,17 +315,20 @@
                     cast_copy(which, chunk, child).start()
 
             if which == 1:
-
-                @pl.when(core == 1)
-                def _():
-                    part_copy(chunk).start()
-
-    forward(1)
-    loads[4].wait()
-
-    @pl.when((y > 0) | (core == 1))
-    def _():
+                part_copy(chunk).start()
+                if chunk == 0:
+                    for step in range(1, 2 * chips):
+                        head_copy(step).start()
+
+    def keep_split(ref, value):
+        ref[0], ref[1] = split(value)
+
+    def kept(ref):
+        return ref[0], ref[1]
+
+    def forward_r():
         forward(0)
+        keep_split(bounce_t, buf[FINAL_R].T)
 
     extra_copy = pltpu.make_async_remote_copy(
         src_ref=extra,
@@ -303,9 +339,6 @@
         device_id_type=MESH,
     )
 
-    def keep_split(ref, value):
-        ref[0], ref[1] = split(value)
-
     def chain_copy(chunk):
         return pltpu.make_async_remote_copy(
             src_ref=leave.at[pl.ds(chunk * rows, rows)],
@@ -318,7 +351,7 @@
 
     def hand_copy(chunk):
         return pltpu.make_async_remote_copy(
-            src_ref=handing.at[pl.ds(chunk * rows, rows)],
+            src_ref=field.at[pl.ds(chunk * rows, rows)],
             dst_ref=handed.at[pl.ds(chunk * rows, rows)],
             send_sem=hand_send.at[chunk],
             recv_sem=hand_recv.at[chunk],
@@ -326,51 +359,74 @@
             device_id_type=MESH,
         )
 
+    forward(1)
+    loads[4].wait()
+
     @pl.when(core == 1)
     def _():
-        keep_split(own_t, buf[FINAL_T].T)
-        extra[...] = split_dot(split(field[...]), (own_t[0], own_t[1]))
+        keep_split(pair_t, buf[FINAL_T].T)
+        extra[...] = split_dot(split(field[...]), kept(pair_t))
         extra_copy.start()
+        for chunk in range(CASTS):
+            part_copy(chunk).wait_recv()
+        keep_split(pair_t, buf[PARTNER].T)
+        forward_r()
         for chunk in range(CHUNKS):
             part = pl.ds(chunk * rows, rows)
             hand_copy(chunk).wait_recv()
-            field[part] += handed[part]
+            field[part] += split_dot(split(handed[part]), kept(pair_t))
 
     @pl.when(core == 0)
     def _():
-        keep_split(own_t, buf[FINAL_T].T)
-        for chunk in range(CHUNKS):
+        for chunk in range(CASTS):
             part_copy(chunk).wait_recv()
         keep_split(pair_t, matmul(buf[PARTNER], buf[FINAL_T]).T)
         extra_copy.wait_recv()
-        for chunk in range(CHUNKS):
-            part = pl.ds(chunk * rows, rows)
-
-            @pl.when(y > 0)
-            def _():
+        extra[...] += split_dot(split(field[...]), kept(pair_t))
+
+        @pl.when(y == 0)
+        def _():
+            for chunk in range(CHUNKS):
+                part = pl.ds(chunk * rows, rows)
+                leave[part] = extra[part]
+                chain_copy(chunk).start()
+                hand_copy(chunk).start()
+
+        @pl.when(y > EARLY)
+        def _():
+            forward_r()
+
+        @pl.when(y > 0)
+        def _():
+            for chunk in range(CHUNKS):
+                part = pl.ds(chunk * rows, rows)
                 chain_copy(chunk).wait_recv()
+
+                @pl.when(y < chips - 1)
+                def _():
+                    leave[part] = extra[part] + split_dot(split(arrive[part]), kept(pair_t))
+                    chain_copy(chunk).start()
+
                 field[part] += arrive[part]
-
-            halves = split(field[part])
-
-            @pl.when(y < chips - 1)
-            def _():
-                leave[part] = split_dot(halves, (pair_t[0], pair_t[1])) + extra[part]
-                chain_copy(chunk).start()
-
-            handing[part] = split_dot(halves, (own_t[0], own_t[1]))
-            hand_copy(chunk).start()
+                hand_copy(chunk).start()
+
+        @pl.when(y <= EARLY)
+        def _():
+            forward_r()
 
     store_down = pltpu.make_async_copy(field, down.at[0], store_sem.at[0])
     store_down.start()
 
-    @pl.when((y == 0) & (core == 0))
-    def _():
-        forward(0)
-
-    arrive[...] = matmul(field[...], buf[FINAL_R].T)
-    store_bounced = pltpu.make_async_copy(arrive, bounced.at[0], store_sem.at[1])
+    handing[...] = split_dot(split(field[...]), kept(bounce_t))
+    store_bounced = pltpu.make_async_copy(handing, bounced.at[0], store_sem.at[1])
     store_bounced.start()
+
+    heads[0] = buf[FINAL_T, pl.ds(0, 8), pl.ds(0, 128)]
+    for step in range(1, 2 * chips):
+        head_copy(step).wait()
+    mark[...] = sum(heads[step] for step in range(2 * chips)) * 0.0
+    store_mark = pltpu.make_async_copy(mark, settled, store_sem.at[2])
+    store_mark.start()
 
     for level in range(LEVELS):
         for number in range(len(routes[level])):
@@ -382,18 +438,19 @@
                     copy.wait_send()
 
     for which in range(2):
-        for chunk in range(CHUNKS):
+        for chunk in range(CASTS):
             for child in range(4):
 
                 @pl.when(children[child][0])
                 def _():
                     cast_copy(which, chunk, child).wait_send()
 
+    for chunk in range(CASTS):
+        part_copy(chunk).wait_send()
+
     @pl.when(core == 1)
     def _():
         extra_copy.wait_send()
-        for chunk in range(CHUNKS):
-            part_copy(chunk).wait_send()
 
     @pl.when(core == 0)
     def _():
@@ -407,37 +464,52 @@
 
     store_down.wait()
     store_bounced.wait()
-
-
-def shards(slabs, incident):
+    store_mark.wait()
+
+
+def layers(doublings, slabs, incident):
     order = slabs.shape[-1]
     rows = incident.shape[1]
+    depth = lax.axis_size("depth")
     block = jax.ShapeDtypeStruct(incident.shape, F32)
     matrix = pltpu.VMEM((order, order), F32)
     halves = pltpu.VMEM((2, order, order), BF16)
     fields = pltpu.VMEM((rows, order), F32)
     dma = pltpu.SemaphoreType.DMA
     return pl.pallas_call(
-        kernel,
-        out_shape=(block, block),
+        functools.partial(kernel, doublings),
+        out_shape=(block, block, jax.ShapeDtypeStruct((8, 128), F32)),
         in_specs=[pl.BlockSpec(memory_space=pl.ANY)] * 2,
-        out_specs=[pl.BlockSpec(memory_space=pl.ANY)] * 2,
+        out_specs=[pl.BlockSpec(memory_space=pl.ANY)] * 3,
         scratch_shapes=[
             pltpu.VMEM((BLOCKS, order, order), F32),
             matrix, matrix, matrix,
             fields, fields, fields, fields, fields, fields,
             halves, halves,
-            dma((5,)), dma((2,)),
+            dma((5,)), dma((3,)),
             dma((LEVELS, 2, 2)), dma((LEVELS, 3, 2)),
-            dma((2, CHUNKS, 4)), dma((2, CHUNKS)),
+            dma((2, CASTS, 4)), dma((2, CASTS)),
             dma((CHUNKS,)), dma((CHUNKS,)),
             dma((CHUNKS,)), dma((CHUNKS,)),
             dma, dma,
-            dma((CHUNKS,)), dma((CHUNKS,)),
+            dma((CASTS,)), dma((CASTS,)),
+            pltpu.VMEM((depth, 8, 128), F32), pltpu.VMEM((8, 128), F32),
+            dma((depth,)), dma((depth,)),
         ],
-        compiler_params=pltpu.CompilerParams(collective_id=0, has_side_effects=True, vmem_limit_bytes=60 * 2**20),
-        name="layers",
+        compiler_params=pltpu.CompilerParams(
+            collective_id=int(doublings > DOUBLINGS), has_side_effects=True, vmem_limit_bytes=60 * 2**20
+        ),
+        name=f"layers{doublings}",
     )(slabs, incident)
+
+
+def shards(slabs, incident):
+    down, bounced, settled = layers(DOUBLINGS, slabs, incident)
+    return lax.cond(
+        settled[0, 0] == 0.0,
+        lambda: (down, bounced),
+        lambda: tuple(layers(MORE_DOUBLINGS, slabs, incident)[:2]),
+    )
 
 
 def solution(mesh):

time: 147 us -> 269 us (1.83)
  the two profiles are of different devices: /device:TPU:63 before, /device:TPU:383 now
where the time goes in v2:
time: 269 us; the launch traced here: 268 us
  Pallas kernels  264 us (98%)
    pallas_call x2, Pallas kernels, layers(): pl.pallas_call(functools.partial(kernel, doublings), out_shape=(block, bl...  264 us

profile of v2, /device:TPU:383, one launch (start us, length us, event | category | flops | bytes accessed | tf_op | source)
XLA Modules:
  0.0 268.4 jit_solution(245050205462076469)
XLA Ops:
  0.6 0.0 copy-start
  0.6 0.0 copy-start.1
  0.6 103.5 %layers3.1 = (f32[1,256,256]{2,1,0:T(8,128)S(1)}, f32[1,256,256]{2,1,0:T(8,128)S(1)}, f32[8,128]{1,0:T(8,128)}) custom-call(f32[1,1,4,256,256]{4,3,2,1,0:T(8,128)} %slabs.1, f32[1,256,256]{2,1,0:T(8,128)} %incident.1), custom_call_target="tpu_custom_call" | custom-call | tf_op jit(solution)/shard_map/layers3/pallas_call | solution.py:479
  104.2 1.2 slice.3
  106.0 0.0 copy-done
  106.0 0.0 copy-done.1
  106.0 160.9 %conditional.1 = ((f32[1,256,256]{2,1,0:T(8,128)S(1)}, f32[1,256,256]{2,1,0:T(8,128)S(1)})) conditional(s32[]{:T(128)} %bitcast, (f32[1,1,4,256,256]{4,3,2,1,0:T(8,128)S(1)}, f32[1,256,256]{2,1,0:T(8,128)S(1)}) %tuple.23, (f32[1,256,256]{2,1,0:T(8,128)S(1)}, f32[1,256,256]{2,1,0:T(8,128)S(1)}) %tuple.15), branch_computations={%region_0.0_spmd, %region_1.0_spmd} | conditional | bytes 24 | solution.py:508
  106.2 160.5 %layers24.1 = (f32[1,256,256]{2,1,0:T(8,128)S(1)}, f32[1,256,256]{2,1,0:T(8,128)S(1)}, f32[8,128]{1,0:T(8,128)}) custom-call(f32[1,1,4,256,256]{4,3,2,1,0:T(8,128)S(1)} %get-tuple-element.8.slabs, f32[1,256,256]{2,1,0:T(8,128)S(1)} %get-tuple-element.9.incident), custom_call_target="tpu_custom_call" | custom-call | tf_op jit(solution)/shard_map/cond/branch_0_fun/layers24/pallas_call | solution.py:479
  267.0 0.7 copy.10
  267.7 0.7 copy.11
Async XLA Ops:
  0.6 105.4 %copy-start = (f32[1,1,4,256,256]{4,3,2,1,0:T(8,128)S(1)}, f32[1,1,4,256,256]{4,3,2,1,0:T(8,128)}, u32[]{:S(2)}) copy-start(f32[1,1,4,256,256]{4,3,2,1,0:T(8,128)} %slabs.1) | copy-start | bytes 3145732
  0.6 105.4 %copy-start.1 = (f32[1,256,256]{2,1,0:T(8,128)S(1)}, f32[1,256,256]{2,1,0:T(8,128)}, u32[]{:S(2)}) copy-start(f32[1,256,256]{2,1,0:T(8,128)} %incident.1) | copy-start | bytes 786436

commit v3 on v2

--- a/solution.py
+++ b/solution.py
@@ -12,7 +12,7 @@
 MESH = pl.DeviceIdType.MESH
 DOUBLINGS = 3
 MORE_DOUBLINGS = 24
-REMAINDER = 1e-6
+REMAINDER = 1e-5
 CHUNKS = 8
 CASTS = 8
 ROOT_Z = 1
@@ -47,7 +47,7 @@
     buf, power, inverse, coupled, field, arrive, leave, handed, handing, extra, pair_t, bounce_t,
     load_sem, store_sem, tree_send, tree_recv, cast_send, cast_recv,
     chain_send, chain_recv, hand_send, hand_recv, extra_send, extra_recv, part_send, part_recv,
-    heads, mark, head_send, head_recv,
+    heads, poison, relay_send, relay_recv,
 ):
     slab = lax.axis_index("slab")
     depth = lax.axis_index("depth")
@@ -87,12 +87,10 @@
     merged2 = (on_rt & (z2 == 0)) | (on_qu & (z2 == 1))
     inner3 = (on_qu & (z4 == 1)) | (on_rt & (z4 == 2))
     ahead3 = jnp.where(z4 < 2, 1, -1)
-    root = on_rt & (z == root_z)
-    rt_rows = [row for row in (1, 5) if row != root_z]
-    sources = [(rt_x, row) for row in rt_rows] + [(qu_x, 2)]
-    source4 = on_qu & (z == 2)
-    for row in rt_rows:
-        source4 = source4 | (on_rt & (z == row))
+    row = z == root_z
+    root = row & (on_rt | on_qu)
+    from_qu = on_qu & (z == root_z + 1)
+    from_rt = on_rt & (z == root_z + 4)
 
     barrier = pltpu.get_barrier_semaphore()
 
@@ -101,23 +99,34 @@
 
     for px, pz in ((1, 0), (-1, 0), (2, 0), (0, 1), (0, -1)):
         greet(slab=at(x + px, z + pz))
-    for step in range(1, 2 * chips):
-        greet(depth=lax.rem(depth + step, 2 * chips))
-
-    @pl.when(source4)
-    def _():
-        greet(slab=at(rt_x, root_z))
-
-    @pl.when(root)
-    def _():
-        for px, pz in sources:
-            greet(slab=at(px, pz))
-
-    met = [source4] + [root] * len(sources)
-    pl.semaphore_wait(barrier, 4 + 2 * chips + sum(flag.astype(jnp.int32) for flag in met))
+    greet(depth=depth + 1 - 2 * core)
+
+    @pl.when(y > 0)
+    def _():
+        greet(depth=depth - 2)
+
+    @pl.when(y < chips - 1)
+    def _():
+        greet(depth=depth + 2)
+
+    meetings = [
+        (from_qu, at(rt_x, root_z)),
+        (from_rt, at(rt_x, root_z)),
+        (from_rt, at(qu_x, root_z)),
+        (root & on_rt, at(qu_x, root_z + 1)),
+        (root & on_rt, at(rt_x, root_z + 4)),
+        (root & on_qu, at(rt_x, root_z + 4)),
+    ]
+    for meets, target in meetings:
+
+        @pl.when(meets)
+        def _(target=target):
+            greet(slab=target)
+
+    met = [y > 0, y < chips - 1] + [meets for meets, _ in meetings]
+    pl.semaphore_wait(barrier, 6 + sum(flag.astype(jnp.int32) for flag in met))
 
     true = x >= 0
-    false = x < 0
     routes = [
         [(true, at(x + 1 - 2 * lax.rem(x, 2), z), 2)],
         [
@@ -133,7 +142,8 @@
             (merged2, at(x, z + ahead3), jnp.where(inner3, 2, 0)),
         ],
         [
-            (source4, at(rt_x, root_z), jnp.where(on_qu, 1, jnp.where(z == 1, 0, 2))),
+            (from_qu | from_rt, at(rt_x, root_z), jnp.where(on_qu, 1, 2)),
+            (from_qu | from_rt | (root & on_rt), at(qu_x, root_z), jnp.where(on_qu, 1, jnp.where(row, 0, 2))),
         ],
     ]
     computes = [
@@ -143,7 +153,7 @@
         (on_rt & (z4 == 1)) | (on_qu & (z4 == 2)),
         root,
     ]
-    local = [3, 1 - core, 0, 3, {1: 0, 5: 2}.get(ROOT_Z, 3)]
+    local = [3, 1 - core, 0, 3, jnp.where(on_rt, 0, 3)]
 
     def tree_copy(level, number, part, source):
         sends, target, pair = routes[level][number]
@@ -227,8 +237,8 @@
         if doublings <= DOUBLINGS:
             for _ in range(doublings - 1):
                 double(split(power[...]))
-            left = jnp.sum(jnp.square(power[...]), axis=(0, 1), keepdims=True)
-            inverse[...] += jnp.where(left < REMAINDER, 0.0, jnp.nan)
+            last = jnp.square(power[...]).reshape(order // 8, 8, order // 128, 128)
+            poison[...] = jnp.where(jnp.sum(last, axis=(0, 2)) < REMAINDER / 1024, 0.0, jnp.nan)
         else:
 
             def step(_, carry):
@@ -242,15 +252,31 @@
         right = split(buf[operand(level, 0, 1)])
         through = split_dot(solved, right)
         turned = split_dot(split(coupled[...]), right)
-        arrived(level, 1, 1)
-        arrived(level, 0, 0)
-        buf[slot(level, 3, 0)] = buf[operand(level, 0, 0)] + matmul(buf[operand(level, 1, 1)], turned)
+        head = (pl.ds(0, 8), pl.ds(0, 128))
+
+        def finish(part, value):
+            place = slot(level, 3, part)
+            buf[place] = value
+            if doublings <= DOUBLINGS:
+                buf[(place, *head)] += poison[...]
+            if level + 1 < LEVELS:
+                send_part(level + 1, part, place)
+
+        def reflection():
+            arrived(level, 1, 1)
+            arrived(level, 0, 0)
+            finish(0, buf[operand(level, 0, 0)] + matmul(buf[operand(level, 1, 1)], turned))
+
+        def transmission():
+            arrived(level, 2, 1)
+            finish(1, matmul(buf[operand(level, 2, 1)], through))
+
         if level + 1 < LEVELS:
-            send_part(level + 1, 0, slot(level, 3, 0))
-        arrived(level, 2, 1)
-        buf[slot(level, 3, 1)] = matmul(buf[operand(level, 2, 1)], through)
-        if level + 1 < LEVELS:
-            send_part(level + 1, 1, slot(level, 3, 1))
+            reflection()
+            transmission()
+        else:
+            transmission()
+            reflection()
 
     for level in range(LEVELS):
 
@@ -258,14 +284,12 @@
         def _(level=level):
             merge(level)
 
-    dx = lax.rem(x - rt_x + 4, 4)
     dz = lax.rem(z - root_z + 8, 8)
-    x_first = core == 0
-    x_line = jnp.logical_not(x_first) | (dz == 0)
-    z_line = x_first | (dx == 0)
+    on_pair = on_rt | on_qu
+    x_line = (core == 1) | row
+    z_line = (core == 0) | on_pair
     children = [
-        (x_line & ((dx == 0) | (x_first & (dx == 1))), at(x + 1, z)),
-        (x_line & ((dx == 0) | (jnp.logical_not(x_first) & (dx == 3))), at(x - 1, z)),
+        (on_pair & x_line, at(x + 1 - 2 * lax.rem(x, 2), z)),
         (z_line & (dz <= 3), at(x, z + 1)),
         (z_line & ((dz == 0) | (dz >= 6)), at(x, z - 1)),
     ]
@@ -291,15 +315,32 @@
             device_id_type=MESH,
         )
 
-    def head_copy(step):
+    def relay_copy(way):
         return pltpu.make_async_remote_copy(
-            src_ref=buf.at[FINAL_T, pl.ds(0, 8), pl.ds(0, 128)],
-            dst_ref=heads.at[step],
-            send_sem=head_send.at[step],
-            recv_sem=head_recv.at[step],
-            device_id={"depth": lax.rem(depth + step, 2 * chips)},
+            src_ref=heads.at[way],
+            dst_ref=heads.at[2 + way],
+            send_sem=relay_send.at[way],
+            recv_sem=relay_recv.at[way],
+            device_id={"depth": lax.rem(depth + (2 * chips - 2 if way else 2), 2 * chips)},
             device_id_type=MESH,
         )
+
+    first = y == 0
+    final = y == chips - 1
+
+    def relay(way):
+        head = (pl.ds(0, 8), pl.ds(0, 128))
+        start, end = (final, first) if way else (first, final)
+        heads[way] = (buf[(FINAL_T, *head)] + buf[(PARTNER, *head)]) * 0.0
+
+        @pl.when(jnp.logical_not(start))
+        def _():
+            relay_copy(way).wait_recv()
+            heads[way] += heads[2 + way]
+
+        @pl.when(jnp.logical_not(end))
+        def _():
+            relay_copy(way).start()
 
     def forward(which):
         for chunk in range(CASTS):
@@ -308,7 +349,7 @@
             def _():
                 cast_copy(which, chunk, 0).wait_recv()
 
-            for child in range(4):
+            for child in range(3):
 
                 @pl.when(children[child][0])
                 def _():
@@ -316,9 +357,6 @@
 
             if which == 1:
                 part_copy(chunk).start()
-                if chunk == 0:
-                    for step in range(1, 2 * chips):
-                        head_copy(step).start()
 
     def keep_split(ref, value):
         ref[0], ref[1] = split(value)
@@ -370,12 +408,23 @@
         for chunk in range(CASTS):
             part_copy(chunk).wait_recv()
         keep_split(pair_t, buf[PARTNER].T)
+
+        @pl.when(y >= chips // 2)
+        def _():
+            relay(1)
+
         forward_r()
         for chunk in range(CHUNKS):
             part = pl.ds(chunk * rows, rows)
             hand_copy(chunk).wait_recv()
             field[part] += split_dot(split(handed[part]), kept(pair_t))
 
+        relay(0)
+
+        @pl.when(y < chips // 2)
+        def _():
+            relay(1)
+
     @pl.when(core == 0)
     def _():
         for chunk in range(CASTS):
@@ -392,6 +441,10 @@
                 chain_copy(chunk).start()
                 hand_copy(chunk).start()
 
+        @pl.when(y >= chips // 2)
+        def _():
+            relay(1)
+
         @pl.when(y > EARLY)
         def _():
             forward_r()
@@ -410,9 +463,15 @@
                 field[part] += arrive[part]
                 hand_copy(chunk).start()
 
+        relay(0)
+
         @pl.when(y <= EARLY)
         def _():
             forward_r()
+
+        @pl.when(y < chips // 2)
+        def _():
+            relay(1)
 
     store_down = pltpu.make_async_copy(field, down.at[0], store_sem.at[0])
     store_down.start()
@@ -421,12 +480,7 @@
     store_bounced = pltpu.make_async_copy(handing, bounced.at[0], store_sem.at[1])
     store_bounced.start()
 
-    heads[0] = buf[FINAL_T, pl.ds(0, 8), pl.ds(0, 128)]
-    for step in range(1, 2 * chips):
-        head_copy(step).wait()
-    mark[...] = sum(heads[step] for step in range(2 * chips)) * 0.0
-    store_mark = pltpu.make_async_copy(mark, settled, store_sem.at[2])
-    store_mark.start()
+    settled[0, 0] = jnp.sum(heads[0] + heads[1])
 
     for level in range(LEVELS):
         for number in range(len(routes[level])):
@@ -439,7 +493,7 @@
 
     for which in range(2):
         for chunk in range(CASTS):
-            for child in range(4):
+            for child in range(3):
 
                 @pl.when(children[child][0])
                 def _():
@@ -462,15 +516,21 @@
             for chunk in range(CHUNKS):
                 chain_copy(chunk).wait_send()
 
+    @pl.when(jnp.logical_not(final))
+    def _():
+        relay_copy(0).wait_send()
+
+    @pl.when(jnp.logical_not(first))
+    def _():
+        relay_copy(1).wait_send()
+
     store_down.wait()
     store_bounced.wait()
-    store_mark.wait()
 
 
 def layers(doublings, slabs, incident):
     order = slabs.shape[-1]
     rows = incident.shape[1]
-    depth = lax.axis_size("depth")
     block = jax.ShapeDtypeStruct(incident.shape, F32)
     matrix = pltpu.VMEM((order, order), F32)
     halves = pltpu.VMEM((2, order, order), BF16)
@@ -478,23 +538,23 @@
     dma = pltpu.SemaphoreType.DMA
     return pl.pallas_call(
         functools.partial(kernel, doublings),
-        out_shape=(block, block, jax.ShapeDtypeStruct((8, 128), F32)),
+        out_shape=(block, block, jax.ShapeDtypeStruct((1, 1), F32)),
         in_specs=[pl.BlockSpec(memory_space=pl.ANY)] * 2,
-        out_specs=[pl.BlockSpec(memory_space=pl.ANY)] * 3,
+        out_specs=[pl.BlockSpec(memory_space=pl.ANY)] * 2 + [pl.BlockSpec(memory_space=pltpu.SMEM)],
         scratch_shapes=[
             pltpu.VMEM((BLOCKS, order, order), F32),
             matrix, matrix, matrix,
             fields, fields, fields, fields, fields, fields,
             halves, halves,
-            dma((5,)), dma((3,)),
+            dma((5,)), dma((2,)),
             dma((LEVELS, 2, 2)), dma((LEVELS, 3, 2)),
-            dma((2, CASTS, 4)), dma((2, CASTS)),
+            dma((2, CASTS, 3)), dma((2, CASTS)),
             dma((CHUNKS,)), dma((CHUNKS,)),
             dma((CHUNKS,)), dma((CHUNKS,)),
             dma, dma,
             dma((CASTS,)), dma((CASTS,)),
-            pltpu.VMEM((depth, 8, 128), F32), pltpu.VMEM((8, 128), F32),
-            dma((depth,)), dma((depth,)),
+            pltpu.VMEM((4, 8, 128), F32), pltpu.VMEM((8, 128), F32),
+            dma((2,)), dma((2,)),
         ],
         compiler_params=pltpu.CompilerParams(
             collective_id=int(doublings > DOUBLINGS), has_side_effects=True, vmem_limit_bytes=60 * 2**20

time: 269 us -> 273 us (1.015)
  Pallas kernels: 264 us -> 270 us
    pallas_call x2, Pallas kernels: 264 us -> 270 us  [layers(): pl.pallas_call(functools.partial(kernel, doublings), out_shape=(block, bl...]
where the time goes in v3:
time: 273 us
  Pallas kernels  270 us (99%)
    pallas_call x2, Pallas kernels, layers(): pl.pallas_call(functools.partial(kernel, doublings), out_shape=(block, bl...  270 us

profile of v3, /device:TPU:383, one launch (start us, length us, event | category | flops | bytes accessed | tf_op | source)
XLA Modules:
  0.0 272.5 jit_solution(14470765558469374585)
XLA Ops:
  0.6 0.0 copy-start
  0.6 0.0 copy-start.1
  0.6 107.7 %layers3.1 = (f32[1,256,256]{2,1,0:T(8,128)S(1)}, f32[1,256,256]{2,1,0:T(8,128)S(1)}, f32[1,1]{1,0:T(1,128)}) custom-call(f32[1,1,4,256,256]{4,3,2,1,0:T(8,128)} %slabs.1, f32[1,256,256]{2,1,0:T(8,128)} %incident.1), custom_call_target="tpu_custom_call" | custom-call | tf_op jit(solution)/shard_map/layers3/pallas_call | solution.py:539
  109.0 0.0 copy-done
  109.0 0.0 copy-done.1
  109.0 162.1 %conditional.1 = ((f32[1,256,256]{2,1,0:T(8,128)S(1)}, f32[1,256,256]{2,1,0:T(8,128)S(1)})) conditional(s32[]{:T(128)} %bitcast, (f32[1,1,4,256,256]{4,3,2,1,0:T(8,128)S(1)}, f32[1,256,256]{2,1,0:T(8,128)S(1)}) %tuple.23, (f32[1,256,256]{2,1,0:T(8,128)S(1)}, f32[1,256,256]{2,1,0:T(8,128)S(1)}) %tuple.15), branch_computations={%region_0.0_spmd, %region_1.0_spmd} | conditional | bytes 24 | solution.py:568
  109.0 162.1 %layers24.1 = (f32[1,256,256]{2,1,0:T(8,128)S(1)}, f32[1,256,256]{2,1,0:T(8,128)S(1)}, f32[1,1]{1,0:T(1,128)}) custom-call(f32[1,1,4,256,256]{4,3,2,1,0:T(8,128)S(1)} %get-tuple-element.8.slabs, f32[1,256,256]{2,1,0:T(8,128)S(1)} %get-tuple-element.9.incident), custom_call_target="tpu_custom_call" | custom-call | tf_op jit(solution)/shard_map/cond/branch_0_fun/layers24/pallas_call | solution.py:539
  271.1 0.7 copy.10
  271.8 0.7 copy.11
Async XLA Ops:
  0.6 108.4 %copy-start = (f32[1,1,4,256,256]{4,3,2,1,0:T(8,128)S(1)}, f32[1,1,4,256,256]{4,3,2,1,0:T(8,128)}, u32[]{:S(2)}) copy-start(f32[1,1,4,256,256]{4,3,2,1,0:T(8,128)} %slabs.1) | copy-start | bytes 3145732
  0.6 108.4 %copy-start.1 = (f32[1,256,256]{2,1,0:T(8,128)S(1)}, f32[1,256,256]{2,1,0:T(8,128)}, u32[]{:S(2)}) copy-start(f32[1,256,256]{2,1,0:T(8,128)} %incident.1) | copy-start | bytes 786436

commit v4 on v3

--- a/solution.py
+++ b/solution.py
@@ -21,6 +21,8 @@
 OWN = 8 * LEVELS
 PARTNER = OWN + 4
 BLOCKS = OWN + 5
+TAKEN = 2
+KEPT = 0
 FINAL_R = 8 * (LEVELS - 1) + 6
 FINAL_T = FINAL_R + 1
 
@@ -47,7 +49,7 @@
     buf, power, inverse, coupled, field, arrive, leave, handed, handing, extra, pair_t, bounce_t,
     load_sem, store_sem, tree_send, tree_recv, cast_send, cast_recv,
     chain_send, chain_recv, hand_send, hand_recv, extra_send, extra_recv, part_send, part_recv,
-    heads, poison, relay_send, relay_recv,
+    heads, poison, relay_send, relay_recv, give_send, give_recv,
 ):
     slab = lax.axis_index("slab")
     depth = lax.axis_index("depth")
@@ -77,18 +79,20 @@
     def slot(level, pair, part):
         return level * 8 + pair * 2 + part
 
-    outer = (x == 0) | (x == 3)
     on_rt = x == rt_x
     on_qu = x == qu_x
     z2 = lax.rem(z, 2)
     z4 = lax.rem(z, 4)
     mirror = at(3 - x, z)
+    odd = lax.rem(x, 2) == 1
+    beside = at(x + 1 - 2 * lax.rem(x, 2), z)
+    takes = on_rt | on_qu
     crossing2 = (on_qu & (z2 == 0)) | (on_rt & (z2 == 1))
     merged2 = (on_rt & (z2 == 0)) | (on_qu & (z2 == 1))
     inner3 = (on_qu & (z4 == 1)) | (on_rt & (z4 == 2))
     ahead3 = jnp.where(z4 < 2, 1, -1)
     row = z == root_z
-    root = row & (on_rt | on_qu)
+    root = row & on_rt
     from_qu = on_qu & (z == root_z + 1)
     from_rt = on_rt & (z == root_z + 4)
 
@@ -97,7 +101,7 @@
     def greet(**target):
         pl.semaphore_signal(barrier, inc=1, device_id=target, device_id_type=MESH)
 
-    for px, pz in ((1, 0), (-1, 0), (2, 0), (0, 1), (0, -1)):
+    for px, pz in ((1, 0), (-1, 0), (0, 1), (0, -1)):
         greet(slab=at(x + px, z + pz))
     greet(depth=depth + 1 - 2 * core)
 
@@ -112,10 +116,8 @@
     meetings = [
         (from_qu, at(rt_x, root_z)),
         (from_rt, at(rt_x, root_z)),
-        (from_rt, at(qu_x, root_z)),
-        (root & on_rt, at(qu_x, root_z + 1)),
-        (root & on_rt, at(rt_x, root_z + 4)),
-        (root & on_qu, at(rt_x, root_z + 4)),
+        (root, at(qu_x, root_z + 1)),
+        (root, at(rt_x, root_z + 4)),
     ]
     for meets, target in meetings:
 
@@ -124,15 +126,11 @@
             greet(slab=target)
 
     met = [y > 0, y < chips - 1] + [meets for meets, _ in meetings]
-    pl.semaphore_wait(barrier, 6 + sum(flag.astype(jnp.int32) for flag in met))
-
-    true = x >= 0
+    pl.semaphore_wait(barrier, 5 + sum(flag.astype(jnp.int32) for flag in met))
+
     routes = [
-        [(true, at(x + 1 - 2 * lax.rem(x, 2), z), 2)],
-        [
-            (jnp.logical_not(outer), jnp.where(core == 0, mirror, at(x + 2, z)), 2),
-            (outer == (core == 0), at(x + 1 - 2 * lax.rem(x, 2), z), core),
-        ],
+        [],
+        [(takes, mirror, 2)],
         [
             (crossing2, mirror, 1),
             (crossing2, at(x, z + 1 - 2 * z2), 2),
@@ -143,17 +141,16 @@
         ],
         [
             (from_qu | from_rt, at(rt_x, root_z), jnp.where(on_qu, 1, 2)),
-            (from_qu | from_rt | (root & on_rt), at(qu_x, root_z), jnp.where(on_qu, 1, jnp.where(row, 0, 2))),
         ],
     ]
     computes = [
-        true,
-        on_rt | on_qu,
+        takes,
+        takes,
         merged2,
         (on_rt & (z4 == 1)) | (on_qu & (z4 == 2)),
         root,
     ]
-    local = [3, 1 - core, 0, 3, jnp.where(on_rt, 0, 3)]
+    local = [3, 3, 0, 3, 0]
 
     def tree_copy(level, number, part, source):
         sends, target, pair = routes[level][number]
@@ -186,43 +183,31 @@
 
     for load in loads[:4]:
         load.wait()
-    odd = lax.rem(x, 2) == 1
-    first_pair = jnp.where(odd, OWN, OWN + 2)
-    add_pair = jnp.where(odd, OWN + 2, OWN)
-    send_part(0, 0, first_pair)
-    send_part(0, 1, first_pair + 1)
-
-    def operand(level, pair, part):
-        if level == 0:
-            if pair == 2:
-                return slot(0, 2, part)
-            return (add_pair if pair == 0 else first_pair) + part
-        own = slot(level - 1, 3, part)
-        known = local[level]
-        if isinstance(known, int):
-            return own if known == pair else slot(level, pair, part)
-        return jnp.where(known == pair, own, slot(level, pair, part))
-
-    def arrived(level, pair, part):
-        if level == 0:
-            if pair == 2:
-                await_part(0, 2, part)
-            return
-        known = local[level]
-        if isinstance(known, int):
-            if known != pair:
-                await_part(level, pair, part)
-            return
-
-        @pl.when(known != pair)
-        def _():
-            await_part(level, pair, part)
-
-    def merge(level):
-        arrived(level, 1, 0)
-        arrived(level, 2, 0)
-        near = buf[operand(level, 1, 0)]
-        far = split(buf[operand(level, 2, 0)])
+    second = jnp.where(odd == (core == 0), 1, 3)
+    blocks = [jnp.where(odd, 0, 2), second, 4 - second, jnp.where(odd, 2, 0)]
+
+    def give_copy(turn):
+        return pltpu.make_async_remote_copy(
+            src_ref=buf.at[OWN + blocks[turn]],
+            dst_ref=buf.at[TAKEN + blocks[turn]],
+            send_sem=give_send.at[turn],
+            recv_sem=give_recv.at[turn],
+            device_id={"slab": beside},
+            device_id_type=MESH,
+        )
+
+    @pl.when(jnp.logical_not(takes))
+    def _():
+        for turn in range(4):
+            give_copy(turn).start()
+
+    head = (pl.ds(0, 8), pl.ds(0, 128))
+
+    def merge(place, wait, finish, transmission_first=False):
+        wait("p1")
+        wait("p2")
+        near = buf[place["p1"]]
+        far = split(buf[place["p2"]])
         system = split_dot(split(near), far)
         ones = lax.broadcasted_iota(jnp.int32, (order, order), 0) == lax.broadcasted_iota(jnp.int32, (order, order), 1)
         inverse[...] = system + jnp.where(ones, 1.0, 0.0)
@@ -248,48 +233,104 @@
             lax.fori_loop(0, doublings - 1, step, 0)
         solved = split(inverse[...])
         coupled[...] = split_dot(far, solved)
-        arrived(level, 0, 1)
-        right = split(buf[operand(level, 0, 1)])
+        wait("s")
+        right = split(buf[place["s"]])
         through = split_dot(solved, right)
         turned = split_dot(split(coupled[...]), right)
-        head = (pl.ds(0, 8), pl.ds(0, 128))
-
-        def finish(part, value):
-            place = slot(level, 3, part)
-            buf[place] = value
-            if doublings <= DOUBLINGS:
-                buf[(place, *head)] += poison[...]
-            if level + 1 < LEVELS:
-                send_part(level + 1, part, place)
 
         def reflection():
-            arrived(level, 1, 1)
-            arrived(level, 0, 0)
-            finish(0, buf[operand(level, 0, 0)] + matmul(buf[operand(level, 1, 1)], turned))
+            wait("m1")
+            wait("add")
+            finish(0, buf[place["add"]] + matmul(buf[place["m1"]], turned))
 
         def transmission():
-            arrived(level, 2, 1)
-            finish(1, matmul(buf[operand(level, 2, 1)], through))
-
-        if level + 1 < LEVELS:
+            wait("m2")
+            finish(1, matmul(buf[place["m2"]], through))
+
+        if transmission_first:
+            transmission()
+            reflection()
+        else:
             reflection()
             transmission()
-        else:
-            transmission()
-            reflection()
-
-    for level in range(LEVELS):
+
+    def put(place, value):
+        buf[place] = value
+        if doublings <= DOUBLINGS:
+            buf[(place, *head)] += poison[...]
+
+    upper = jnp.where(odd, TAKEN, OWN)
+    lower = jnp.where(odd, OWN, TAKEN)
+
+    def sides(is_qu):
+        return {
+            "p1": jnp.where(is_qu, lower, upper + 2),
+            "p2": jnp.where(is_qu, upper + 2, lower),
+            "s": jnp.where(is_qu, lower + 3, upper + 1),
+            "add": jnp.where(is_qu, lower + 2, upper),
+            "m1": jnp.where(is_qu, lower + 1, upper + 3),
+            "m2": jnp.where(is_qu, upper + 3, lower + 1),
+        }
+
+    def given(turns):
+        def wait(name):
+            if name in turns:
+                give_copy(turns[name]).wait_recv()
+
+        return wait
+
+    def finish_sent(part, value):
+        put(slot(0, 3, part), value)
+        send_part(1, part, slot(0, 3, part))
+
+    def finish_kept(part, value):
+        put(KEPT + part, value)
+
+    @pl.when(takes & (core == 0))
+    def _():
+        merge(sides(x < 2), given({"p1": 0, "m2": 1}), finish_sent)
+        merge(sides(x >= 2), given({"s": 2, "add": 3}), finish_kept)
+
+    @pl.when(takes & (core == 1))
+    def _():
+        merge(sides(x < 2), given({"p1": 0, "s": 1, "m1": 2, "add": 3}), finish_sent, transmission_first=True)
+        merge(sides(x >= 2), given({}), finish_kept)
+
+    names = {"add": (0, 0), "s": (0, 1), "p1": (1, 0), "m1": (1, 1), "p2": (2, 0), "m2": (2, 1)}
+
+    def merge_level(level):
+        def operand(pair, part):
+            if level == 1:
+                return [KEPT + part, slot(0, 3, part), slot(1, 2, part)][pair]
+            return slot(level - 1, 3, part) if local[level] == pair else slot(level, pair, part)
+
+        def wait(name):
+            pair, part = names[name]
+            if pair == 2 if level == 1 else pair != local[level]:
+                await_part(level, pair, part)
+
+        def finish(part, value):
+            put(slot(level, 3, part), value)
+            if level + 1 < LEVELS:
+                send_part(level + 1, part, slot(level, 3, part))
+
+        place = {name: operand(*key) for name, key in names.items()}
+        merge(place, wait, finish, transmission_first=level + 1 == LEVELS)
+
+    for level in range(1, LEVELS):
 
         @pl.when(computes[level])
         def _(level=level):
-            merge(level)
-
+            merge_level(level)
+
+    dx = lax.rem(x - rt_x + 4, 4)
     dz = lax.rem(z - root_z + 8, 8)
-    on_pair = on_rt | on_qu
-    x_line = (core == 1) | row
-    z_line = (core == 0) | on_pair
+    x_first = core == 0
+    x_line = jnp.logical_not(x_first) | row
+    z_line = x_first | (dx == 0)
     children = [
-        (on_pair & x_line, at(x + 1 - 2 * lax.rem(x, 2), z)),
+        (x_line & ((dx == 0) | (x_first & (dx == 1))), at(x + 1, z)),
+        (x_line & ((dx == 0) | (jnp.logical_not(x_first) & (dx == 3))), at(x - 1, z)),
         (z_line & (dz <= 3), at(x, z + 1)),
         (z_line & ((dz == 0) | (dz >= 6)), at(x, z - 1)),
     ]
@@ -349,7 +390,7 @@
             def _():
                 cast_copy(which, chunk, 0).wait_recv()
 
-            for child in range(3):
+            for child in range(4):
 
                 @pl.when(children[child][0])
                 def _():
@@ -482,6 +523,11 @@
 
     settled[0, 0] = jnp.sum(heads[0] + heads[1])
 
+    @pl.when(jnp.logical_not(takes))
+    def _():
+        for turn in range(4):
+            give_copy(turn).wait_send()
+
     for level in range(LEVELS):
         for number in range(len(routes[level])):
             for part in range(2):
@@ -493,7 +539,7 @@
 
     for which in range(2):
         for chunk in range(CASTS):
-            for child in range(3):
+            for child in range(4):
 
                 @pl.when(children[child][0])
                 def _():
@@ -548,13 +594,14 @@
             halves, halves,
             dma((5,)), dma((2,)),
             dma((LEVELS, 2, 2)), dma((LEVELS, 3, 2)),
-            dma((2, CASTS, 3)), dma((2, CASTS)),
+            dma((2, CASTS, 4)), dma((2, CASTS)),
             dma((CHUNKS,)), dma((CHUNKS,)),
             dma((CHUNKS,)), dma((CHUNKS,)),
             dma, dma,
             dma((CASTS,)), dma((CASTS,)),
             pltpu.VMEM((4, 8, 128), F32), pltpu.VMEM((8, 128), F32),
             dma((2,)), dma((2,)),
+            dma((4,)), dma((4,)),
         ],
         compiler_params=pltpu.CompilerParams(
             collective_id=int(doublings > DOUBLINGS), has_side_effects=True, vmem_limit_bytes=60 * 2**20

time: 273 us -> 268 us (0.982)
  Pallas kernels: 270 us -> 265 us
    pallas_call x2, Pallas kernels: 270 us -> 265 us  [layers(): pl.pallas_call(functools.partial(kernel, doublings), out_shape=(block, bl...]
where the time goes in v4:
time: 268 us
  Pallas kernels  265 us (99%)
    pallas_call x2, Pallas kernels, layers(): pl.pallas_call(functools.partial(kernel, doublings), out_shape=(block, bl...  265 us

profile of v4, /device:TPU:383, one launch (start us, length us, event | category | flops | bytes accessed | tf_op | source)
XLA Modules:
  0.0 267.6 jit_solution(16709412765237697871)
XLA Ops:
  0.6 0.0 copy-start
  0.6 0.0 copy-start.1
  0.6 99.9 %layers3.1 = (f32[1,256,256]{2,1,0:T(8,128)S(1)}, f32[1,256,256]{2,1,0:T(8,128)S(1)}, f32[1,1]{1,0:T(1,128)}) custom-call(f32[1,1,4,256,256]{4,3,2,1,0:T(8,128)} %slabs.1, f32[1,256,256]{2,1,0:T(8,128)} %incident.1), custom_call_target="tpu_custom_call" | custom-call | tf_op jit(solution)/shard_map/layers3/pallas_call | solution.py:585
  101.2 0.0 copy-done
  101.3 0.0 copy-done.1
  101.3 164.9 %conditional.1 = ((f32[1,256,256]{2,1,0:T(8,128)S(1)}, f32[1,256,256]{2,1,0:T(8,128)S(1)})) conditional(s32[]{:T(128)} %bitcast, (f32[1,1,4,256,256]{4,3,2,1,0:T(8,128)S(1)}, f32[1,256,256]{2,1,0:T(8,128)S(1)}) %tuple.23, (f32[1,256,256]{2,1,0:T(8,128)S(1)}, f32[1,256,256]{2,1,0:T(8,128)S(1)}) %tuple.15), branch_computations={%region_0.0_spmd, %region_1.0_spmd} | conditional | bytes 24 | solution.py:615
  101.3 164.9 %layers24.1 = (f32[1,256,256]{2,1,0:T(8,128)S(1)}, f32[1,256,256]{2,1,0:T(8,128)S(1)}, f32[1,1]{1,0:T(1,128)}) custom-call(f32[1,1,4,256,256]{4,3,2,1,0:T(8,128)S(1)} %get-tuple-element.8.slabs, f32[1,256,256]{2,1,0:T(8,128)S(1)} %get-tuple-element.9.incident), custom_call_target="tpu_custom_call" | custom-call | tf_op jit(solution)/shard_map/cond/branch_0_fun/layers24/pallas_call | solution.py:585
  266.2 0.7 copy.10
  266.9 0.7 copy.11
Async XLA Ops:
  0.6 100.6 %copy-start = (f32[1,1,4,256,256]{4,3,2,1,0:T(8,128)S(1)}, f32[1,1,4,256,256]{4,3,2,1,0:T(8,128)}, u32[]{:S(2)}) copy-start(f32[1,1,4,256,256]{4,3,2,1,0:T(8,128)} %slabs.1) | copy-start | bytes 3145732
  0.6 100.6 %copy-start.1 = (f32[1,256,256]{2,1,0:T(8,128)S(1)}, f32[1,256,256]{2,1,0:T(8,128)}, u32[]{:S(2)}) copy-start(f32[1,256,256]{2,1,0:T(8,128)} %incident.1) | copy-start | bytes 786436

commit v5 on v4

--- a/solution.py
+++ b/solution.py
@@ -16,11 +16,14 @@
 CHUNKS = 8
 CASTS = 8
 ROOT_Z = 1
-EARLY = 2
+EARLY = 3
+FIRST_SKIP = 3
 LEVELS = 5
 OWN = 8 * LEVELS
 PARTNER = OWN + 4
-BLOCKS = OWN + 5
+PRODUCT = OWN + 5
+NEXT_PRODUCT = OWN + 6
+BLOCKS = OWN + 7
 TAKEN = 2
 KEPT = 0
 FINAL_R = 8 * (LEVELS - 1) + 6
@@ -46,10 +49,11 @@
 
 def kernel(
     doublings, slabs, incident, down, bounced, settled,
-    buf, power, inverse, coupled, field, arrive, leave, handed, handing, extra, pair_t, bounce_t,
+    buf, power, inverse, coupled, field, arrive, leave, handed, handing, extra, leap, ahead, pair_t, bounce_t, skip_t,
     load_sem, store_sem, tree_send, tree_recv, cast_send, cast_recv,
     chain_send, chain_recv, hand_send, hand_recv, extra_send, extra_recv, part_send, part_recv,
     heads, poison, relay_send, relay_recv, give_send, give_recv,
+    skip_send, back_send, back_recv,
 ):
     slab = lax.axis_index("slab")
     depth = lax.axis_index("depth")
@@ -91,10 +95,18 @@
     merged2 = (on_rt & (z2 == 0)) | (on_qu & (z2 == 1))
     inner3 = (on_qu & (z4 == 1)) | (on_rt & (z4 == 2))
     ahead3 = jnp.where(z4 < 2, 1, -1)
-    row = z == root_z
+    row = lax.rem(z, 4) == root_z
     root = row & on_rt
+    near_root = at(rt_x, root_z)
+    far_root = at(rt_x, root_z + 4)
     from_qu = on_qu & (z == root_z + 1)
-    from_rt = on_rt & (z == root_z + 4)
+    is_near = root & (z == root_z)
+    is_far = root & (z == root_z + 4)
+
+    skips = (core == 0) & (y >= FIRST_SKIP) & (lax.rem(y - FIRST_SKIP, 2) == 0) & (y < chips - 2)
+    skipped = (core == 0) & (y > FIRST_SKIP) & (lax.rem(y - FIRST_SKIP, 2) == 1) & (y < chips - 1)
+    doubles = skips
+    doubled = (core == 0) & (y >= FIRST_SKIP + 2) & (lax.rem(y - FIRST_SKIP, 2) == 0)
 
     barrier = pltpu.get_barrier_semaphore()
 
@@ -114,16 +126,22 @@
         greet(depth=depth + 2)
 
     meetings = [
-        (from_qu, at(rt_x, root_z)),
-        (from_rt, at(rt_x, root_z)),
+        (from_qu, near_root),
+        (from_qu, far_root),
         (root, at(qu_x, root_z + 1)),
-        (root, at(rt_x, root_z + 4)),
+        (is_near, far_root),
+        (is_far, near_root),
+        (doubles, None),
+        (doubled, None),
     ]
     for meets, target in meetings:
 
         @pl.when(meets)
-        def _(target=target):
-            greet(slab=target)
+        def _(target=target, meets=meets):
+            if target is not None:
+                greet(slab=target)
+            else:
+                greet(depth=lax.rem(depth + (4 if meets is doubles else 2 * chips - 4), 2 * chips))
 
     met = [y > 0, y < chips - 1] + [meets for meets, _ in meetings]
     pl.semaphore_wait(barrier, 5 + sum(flag.astype(jnp.int32) for flag in met))
@@ -140,7 +158,8 @@
             (merged2, at(x, z + ahead3), jnp.where(inner3, 2, 0)),
         ],
         [
-            (from_qu | from_rt, at(rt_x, root_z), jnp.where(on_qu, 1, 2)),
+            (from_qu | is_far, near_root, jnp.where(on_qu, 1, 2)),
+            (from_qu | is_near, far_root, jnp.where(on_qu, 1, 0)),
         ],
     ]
     computes = [
@@ -150,7 +169,7 @@
         (on_rt & (z4 == 1)) | (on_qu & (z4 == 2)),
         root,
     ]
-    local = [3, 3, 0, 3, 0]
+    local = [3, 3, 0, 3, None]
 
     def tree_copy(level, number, part, source):
         sends, target, pair = routes[level][number]
@@ -302,10 +321,20 @@
         def operand(pair, part):
             if level == 1:
                 return [KEPT + part, slot(0, 3, part), slot(1, 2, part)][pair]
+            if level == 4:
+                keeps = is_near if pair == 0 else is_far
+                return slot(level, 1, part) if pair == 1 else jnp.where(keeps, slot(3, 3, part), slot(level, pair, part))
             return slot(level - 1, 3, part) if local[level] == pair else slot(level, pair, part)
 
         def wait(name):
             pair, part = names[name]
+            if level == 4 and pair != 1:
+
+                @pl.when(is_far if pair == 0 else is_near)
+                def _():
+                    await_part(level, pair, part)
+
+                return
             if pair == 2 if level == 1 else pair != local[level]:
                 await_part(level, pair, part)
 
@@ -324,15 +353,15 @@
             merge_level(level)
 
     dx = lax.rem(x - rt_x + 4, 4)
-    dz = lax.rem(z - root_z + 8, 8)
+    dz = lax.rem(z - root_z + 4, 4)
     x_first = core == 0
     x_line = jnp.logical_not(x_first) | row
     z_line = x_first | (dx == 0)
     children = [
         (x_line & ((dx == 0) | (x_first & (dx == 1))), at(x + 1, z)),
         (x_line & ((dx == 0) | (jnp.logical_not(x_first) & (dx == 3))), at(x - 1, z)),
-        (z_line & (dz <= 3), at(x, z + 1)),
-        (z_line & ((dz == 0) | (dz >= 6)), at(x, z - 1)),
+        (z_line & (dz <= 1), at(x, z + 1)),
+        (z_line & (dz == 0), at(x, z - 1)),
     ]
 
     def cast_copy(which, chunk, child):
@@ -428,6 +457,27 @@
             device_id_type=MESH,
         )
 
+    def skip_copy(chunk):
+        return pltpu.make_async_remote_copy(
+            src_ref=leap.at[pl.ds(chunk * rows, rows)],
+            dst_ref=arrive.at[pl.ds(chunk * rows, rows)],
+            send_sem=skip_send.at[chunk],
+            recv_sem=chain_recv.at[chunk],
+            device_id={"depth": lax.rem(depth + 4, 2 * chips)},
+            device_id_type=MESH,
+        )
+
+    def back_copy(which):
+        source, target = ((buf.at[PRODUCT], buf.at[NEXT_PRODUCT]), (extra, ahead))[which]
+        return pltpu.make_async_remote_copy(
+            src_ref=source,
+            dst_ref=target,
+            send_sem=back_send.at[which],
+            recv_sem=back_recv.at[which],
+            device_id={"depth": lax.rem(depth + 2 * chips - 2, 2 * chips)},
+            device_id_type=MESH,
+        )
+
     def hand_copy(chunk):
         return pltpu.make_async_remote_copy(
             src_ref=field.at[pl.ds(chunk * rows, rows)],
@@ -470,9 +520,21 @@
     def _():
         for chunk in range(CASTS):
             part_copy(chunk).wait_recv()
-        keep_split(pair_t, matmul(buf[PARTNER], buf[FINAL_T]).T)
+        product = matmul(buf[PARTNER], buf[FINAL_T])
+        buf[PRODUCT] = product
+        keep_split(pair_t, product.T)
+
+        @pl.when(skipped)
+        def _():
+            back_copy(0).start()
+
         extra_copy.wait_recv()
         extra[...] += split_dot(split(field[...]), kept(pair_t))
+
+        @pl.when(skipped)
+        def _():
+            back_copy(1).start()
+
 
         @pl.when(y == 0)
         def _():
@@ -488,7 +550,19 @@
 
         @pl.when(y > EARLY)
         def _():
-            forward_r()
+            forward(0)
+
+        @pl.when(skips)
+        def _():
+            for which in range(2):
+                back_copy(which).wait_recv()
+            keep_split(bounce_t, buf[NEXT_PRODUCT].T)
+            keep_split(skip_t, split_dot(kept(pair_t), kept(bounce_t)))
+            ahead[...] += split_dot(split(extra[...]), kept(bounce_t))
+
+        @pl.when(y > EARLY)
+        def _():
+            keep_split(bounce_t, buf[FINAL_R].T)
 
         @pl.when(y > 0)
         def _():
@@ -496,7 +570,12 @@
                 part = pl.ds(chunk * rows, rows)
                 chain_copy(chunk).wait_recv()
 
-                @pl.when(y < chips - 1)
+                @pl.when(skips)
+                def _():
+                    leap[part] = ahead[part] + split_dot(split(arrive[part]), kept(skip_t))
+                    skip_copy(chunk).start()
+
+                @pl.when((y < chips - 1) & jnp.logical_not(skipped))
                 def _():
                     leave[part] = extra[part] + split_dot(split(arrive[part]), kept(pair_t))
                     chain_copy(chunk).start()
@@ -557,10 +636,20 @@
         for chunk in range(CHUNKS):
             hand_copy(chunk).wait_send()
 
-        @pl.when(y < chips - 1)
+        @pl.when((y < chips - 1) & jnp.logical_not(skipped))
         def _():
             for chunk in range(CHUNKS):
                 chain_copy(chunk).wait_send()
+
+        @pl.when(skips)
+        def _():
+            for chunk in range(CHUNKS):
+                skip_copy(chunk).wait_send()
+
+        @pl.when(skipped)
+        def _():
+            for which in range(2):
+                back_copy(which).wait_send()
 
     @pl.when(jnp.logical_not(final))
     def _():
@@ -590,8 +679,8 @@
         scratch_shapes=[
             pltpu.VMEM((BLOCKS, order, order), F32),
             matrix, matrix, matrix,
-            fields, fields, fields, fields, fields, fields,
-            halves, halves,
+            fields, fields, fields, fields, fields, fields, fields, fields,
+            halves, halves, halves,
             dma((5,)), dma((2,)),
             dma((LEVELS, 2, 2)), dma((LEVELS, 3, 2)),
             dma((2, CASTS, 4)), dma((2, CASTS)),
@@ -602,6 +691,7 @@
             pltpu.VMEM((4, 8, 128), F32), pltpu.VMEM((8, 128), F32),
             dma((2,)), dma((2,)),
             dma((4,)), dma((4,)),
+            dma((CHUNKS,)), dma((2,)), dma((2,)),
         ],
         compiler_params=pltpu.CompilerParams(
             collective_id=int(doublings > DOUBLINGS), has_side_effects=True, vmem_limit_bytes=60 * 2**20

time: 268 us -> 263 us (0.981)
  the two profiles are of different devices: /device:TPU:383 before, /device:TPU:63 now
where the time goes in v5:
time: 263 us; the launch traced here: 261 us
  Pallas kernels  259 us (98%)
    pallas_call x2, Pallas kernels, layers(): pl.pallas_call(functools.partial(kernel, doublings), out_shape=(block, bl...  259 us

profile of v5, /device:TPU:63, one launch (start us, length us, event | category | flops | bytes accessed | tf_op | source)
XLA Modules:
  0.0 261.4 jit_solution(727665758532060983)
XLA Ops:
  0.6 0.0 copy-start
  0.6 0.0 copy-start.1
  0.6 96.1 %layers3.1 = (f32[1,256,256]{2,1,0:T(8,128)S(1)}, f32[1,256,256]{2,1,0:T(8,128)S(1)}, f32[1,1]{1,0:T(1,128)}) custom-call(f32[1,1,4,256,256]{4,3,2,1,0:T(8,128)} %slabs.1, f32[1,256,256]{2,1,0:T(8,128)} %incident.1), custom_call_target="tpu_custom_call" | custom-call | tf_op jit(solution)/shard_map/layers3/pallas_call | solution.py:674
  97.4 0.0 copy-done
  97.5 0.0 copy-done.1
  97.5 162.6 %conditional.1 = ((f32[1,256,256]{2,1,0:T(8,128)S(1)}, f32[1,256,256]{2,1,0:T(8,128)S(1)})) conditional(s32[]{:T(128)} %bitcast, (f32[1,1,4,256,256]{4,3,2,1,0:T(8,128)S(1)}, f32[1,256,256]{2,1,0:T(8,128)S(1)}) %tuple.23, (f32[1,256,256]{2,1,0:T(8,128)S(1)}, f32[1,256,256]{2,1,0:T(8,128)S(1)}) %tuple.15), branch_computations={%region_0.0_spmd, %region_1.0_spmd} | conditional | bytes 24 | solution.py:705
  97.5 162.5 %layers24.1 = (f32[1,256,256]{2,1,0:T(8,128)S(1)}, f32[1,256,256]{2,1,0:T(8,128)S(1)}, f32[1,1]{1,0:T(1,128)}) custom-call(f32[1,1,4,256,256]{4,3,2,1,0:T(8,128)S(1)} %get-tuple-element.8.slabs, f32[1,256,256]{2,1,0:T(8,128)S(1)} %get-tuple-element.9.incident), custom_call_target="tpu_custom_call" | custom-call | tf_op jit(solution)/shard_map/cond/branch_0_fun/layers24/pallas_call | solution.py:674
  260.0 0.7 copy.10
  260.7 0.7 copy.11
Async XLA Ops:
  0.6 96.8 %copy-start = (f32[1,1,4,256,256]{4,3,2,1,0:T(8,128)S(1)}, f32[1,1,4,256,256]{4,3,2,1,0:T(8,128)}, u32[]{:S(2)}) copy-start(f32[1,1,4,256,256]{4,3,2,1,0:T(8,128)} %slabs.1) | copy-start | bytes 3145732
  0.6 96.8 %copy-start.1 = (f32[1,256,256]{2,1,0:T(8,128)S(1)}, f32[1,256,256]{2,1,0:T(8,128)}, u32[]{:S(2)}) copy-start(f32[1,256,256]{2,1,0:T(8,128)} %incident.1) | copy-start | bytes 786436

commit v6 on v4

--- a/solution.py
+++ b/solution.py
@@ -15,7 +15,8 @@
 REMAINDER = 1e-5
 CHUNKS = 8
 CASTS = 8
-ROOT_Z = 1
+NEAR_Z = 2
+FAR_Z = 5
 EARLY = 2
 LEVELS = 5
 OWN = 8 * LEVELS
@@ -74,7 +75,6 @@
 
     rt_x = 1 - core
     qu_x = 2 + core
-    root_z = ROOT_Z
 
     def slot(level, pair, part):
         return level * 8 + pair * 2 + part
@@ -91,18 +91,20 @@
     merged2 = (on_rt & (z2 == 0)) | (on_qu & (z2 == 1))
     inner3 = (on_qu & (z4 == 1)) | (on_rt & (z4 == 2))
     ahead3 = jnp.where(z4 < 2, 1, -1)
-    row = z == root_z
-    root = row & on_rt
-    from_qu = on_qu & (z == root_z + 1)
-    from_rt = on_rt & (z == root_z + 4)
+    near_rt, near_qu, far_root = at(rt_x, NEAR_Z), at(qu_x, NEAR_Z), at(rt_x, FAR_Z)
+    is_near_rt = on_rt & (z == NEAR_Z)
+    is_near_qu = on_qu & (z == NEAR_Z)
+    is_far = on_rt & (z == FAR_Z)
+    is_first = on_rt & (z == 1)
+    root = is_near_rt | is_near_qu | is_far
 
     barrier = pltpu.get_barrier_semaphore()
 
     def greet(**target):
         pl.semaphore_signal(barrier, inc=1, device_id=target, device_id_type=MESH)
 
-    for px, pz in ((1, 0), (-1, 0), (0, 1), (0, -1)):
-        greet(slab=at(x + px, z + pz))
+    for px in (1, 3):
+        greet(slab=at(x + px, z))
     greet(depth=depth + 1 - 2 * core)
 
     @pl.when(y > 0)
@@ -114,10 +116,16 @@
         greet(depth=depth + 2)
 
     meetings = [
-        (from_qu, at(rt_x, root_z)),
-        (from_rt, at(rt_x, root_z)),
-        (root, at(qu_x, root_z + 1)),
-        (root, at(rt_x, root_z + 4)),
+        (is_first, near_qu),
+        (is_first, far_root),
+        (is_near_qu, at(rt_x, 1)),
+        (is_near_qu, far_root),
+        (is_far, at(rt_x, 1)),
+        (is_far, near_qu),
+        (is_far, near_rt),
+        (is_near_rt, far_root),
+        (z > 0, at(x, z - 1)),
+        (z < 7, at(x, z + 1)),
     ]
     for meets, target in meetings:
 
@@ -126,8 +134,9 @@
             greet(slab=target)
 
     met = [y > 0, y < chips - 1] + [meets for meets, _ in meetings]
-    pl.semaphore_wait(barrier, 5 + sum(flag.astype(jnp.int32) for flag in met))
-
+    pl.semaphore_wait(barrier, 3 + sum(flag.astype(jnp.int32) for flag in met))
+
+    final_pair = jnp.where(on_qu, 1, jnp.where(z == 1, 0, 2))
     routes = [
         [],
         [(takes, mirror, 2)],
@@ -140,7 +149,9 @@
             (merged2, at(x, z + ahead3), jnp.where(inner3, 2, 0)),
         ],
         [
-            (from_qu | from_rt, at(rt_x, root_z), jnp.where(on_qu, 1, 2)),
+            (is_first | is_near_qu | is_far, near_rt, final_pair),
+            (is_first | is_far, near_qu, final_pair),
+            (is_first | is_near_qu, far_root, final_pair),
         ],
     ]
     computes = [
@@ -150,7 +161,8 @@
         (on_rt & (z4 == 1)) | (on_qu & (z4 == 2)),
         root,
     ]
-    local = [3, 3, 0, 3, 0]
+    local = [3, 3, 0, 3, 3]
+    holds = [None, is_near_qu, is_far]
 
     def tree_copy(level, number, part, source):
         sends, target, pair = routes[level][number]
@@ -163,13 +175,19 @@
             device_id_type=MESH,
         )
 
+    def send_to(level, number, part, source):
+        sends, copy = tree_copy(level, number, part, source)
+
+        @pl.when(sends)
+        def _():
+            copy.start()
+
     def send_part(level, part, source):
-        for number in range(len(routes[level])):
-            sends, copy = tree_copy(level, number, part, source)
-
-            @pl.when(sends)
-            def _():
-                copy.start()
+        for number in range(min(len(routes[level]), 2)):
+            send_to(level, number, part, source)
+        if len(routes[level]) > 2 and part == 1:
+            send_to(level, 2, 0, source - 1)
+            send_to(level, 2, 1, source)
 
     def await_part(level, pair, part):
         pltpu.make_async_remote_copy(
@@ -302,10 +320,19 @@
         def operand(pair, part):
             if level == 1:
                 return [KEPT + part, slot(0, 3, part), slot(1, 2, part)][pair]
+            if level == 4:
+                return jnp.where(holds[pair], slot(3, 3, part), slot(level, pair, part)) if pair else slot(level, 0, part)
             return slot(level - 1, 3, part) if local[level] == pair else slot(level, pair, part)
 
         def wait(name):
             pair, part = names[name]
+            if level == 4 and pair:
+
+                @pl.when(jnp.logical_not(holds[pair]))
+                def _():
+                    await_part(level, pair, part)
+
+                return
             if pair == 2 if level == 1 else pair != local[level]:
                 await_part(level, pair, part)
 
@@ -323,16 +350,13 @@
         def _(level=level):
             merge_level(level)
 
-    dx = lax.rem(x - rt_x + 4, 4)
-    dz = lax.rem(z - root_z + 8, 8)
-    x_first = core == 0
-    x_line = jnp.logical_not(x_first) | row
-    z_line = x_first | (dx == 0)
+    x_line = (core == 1) | (z == NEAR_Z) | (z == FAR_Z)
+    z_line = (core == 0) | (takes & (z < 4)) | (on_rt & (z >= 4))
     children = [
-        (x_line & ((dx == 0) | (x_first & (dx == 1))), at(x + 1, z)),
-        (x_line & ((dx == 0) | (jnp.logical_not(x_first) & (dx == 3))), at(x - 1, z)),
-        (z_line & (dz <= 3), at(x, z + 1)),
-        (z_line & ((dz == 0) | (dz >= 6)), at(x, z - 1)),
+        (takes & x_line, beside),
+        (on_rt & (z >= 4) & x_line, mirror),
+        (z_line & ((z == NEAR_Z) | (z == FAR_Z) | (z == FAR_Z + 1)), at(x, z + 1)),
+        (z_line & ((z == NEAR_Z) | (z == NEAR_Z - 1) | (z == FAR_Z)), at(x, z - 1)),
     ]
 
     def cast_copy(which, chunk, child):
@@ -593,7 +617,7 @@
             fields, fields, fields, fields, fields, fields,
             halves, halves,
             dma((5,)), dma((2,)),
-            dma((LEVELS, 2, 2)), dma((LEVELS, 3, 2)),
+            dma((LEVELS, 3, 2)), dma((LEVELS, 3, 2)),
             dma((2, CASTS, 4)), dma((2, CASTS)),
             dma((CHUNKS,)), dma((CHUNKS,)),
             dma((CHUNKS,)), dma((CHUNKS,)),

time: 268 us -> 267 us (level)
  the two profiles are of different devices: /device:TPU:383 before, /device:TPU:63 now
where the time goes in v6:
time: 267 us
  Pallas kernels  264 us (99%)
    pallas_call x2, Pallas kernels, layers(): pl.pallas_call(functools.partial(kernel, doublings), out_shape=(block, bl...  264 us

profile of v6, /device:TPU:63, one launch (start us, length us, event | category | flops | bytes accessed | tf_op | source)
XLA Modules:
  0.0 266.9 jit_solution(4082070003479239949)
XLA Ops:
  0.6 0.0 copy-start
  0.6 0.0 copy-start.1
  0.6 105.7 %layers3.1 = (f32[1,256,256]{2,1,0:T(8,128)S(1)}, f32[1,256,256]{2,1,0:T(8,128)S(1)}, f32[1,1]{1,0:T(1,128)}) custom-call(f32[1,1,4,256,256]{4,3,2,1,0:T(8,128)} %slabs.1, f32[1,256,256]{2,1,0:T(8,128)} %incident.1), custom_call_target="tpu_custom_call" | custom-call | tf_op jit(solution)/shard_map/layers3/pallas_call | solution.py:609
  107.0 0.0 copy-done
  107.0 0.0 copy-done.1
  107.0 158.4 %conditional.1 = ((f32[1,256,256]{2,1,0:T(8,128)S(1)}, f32[1,256,256]{2,1,0:T(8,128)S(1)})) conditional(s32[]{:T(128)} %bitcast, (f32[1,1,4,256,256]{4,3,2,1,0:T(8,128)S(1)}, f32[1,256,256]{2,1,0:T(8,128)S(1)}) %tuple.23, (f32[1,256,256]{2,1,0:T(8,128)S(1)}, f32[1,256,256]{2,1,0:T(8,128)S(1)}) %tuple.15), branch_computations={%region_0.0_spmd, %region_1.0_spmd} | conditional | bytes 24 | solution.py:639
  107.0 158.4 %layers24.1 = (f32[1,256,256]{2,1,0:T(8,128)S(1)}, f32[1,256,256]{2,1,0:T(8,128)S(1)}, f32[1,1]{1,0:T(1,128)}) custom-call(f32[1,1,4,256,256]{4,3,2,1,0:T(8,128)S(1)} %get-tuple-element.8.slabs, f32[1,256,256]{2,1,0:T(8,128)S(1)} %get-tuple-element.9.incident), custom_call_target="tpu_custom_call" | custom-call | tf_op jit(solution)/shard_map/cond/branch_0_fun/layers24/pallas_call | solution.py:609
  265.5 0.7 copy.10
  266.2 0.7 copy.11
Async XLA Ops:
  0.6 106.4 %copy-start = (f32[1,1,4,256,256]{4,3,2,1,0:T(8,128)S(1)}, f32[1,1,4,256,256]{4,3,2,1,0:T(8,128)}, u32[]{:S(2)}) copy-start(f32[1,1,4,256,256]{4,3,2,1,0:T(8,128)} %slabs.1) | copy-start | bytes 3145732
  0.6 106.4 %copy-start.1 = (f32[1,256,256]{2,1,0:T(8,128)S(1)}, f32[1,256,256]{2,1,0:T(8,128)}, u32[]{:S(2)}) copy-start(f32[1,256,256]{2,1,0:T(8,128)} %incident.1) | copy-start | bytes 786436

commit v7 on v4

--- a/solution.py
+++ b/solution.py
@@ -15,7 +15,9 @@
 REMAINDER = 1e-5
 CHUNKS = 8
 CASTS = 8
-ROOT_Z = 1
+NEAR_Z = 1
+PIECES = 4
+FAR_Z = 5
 EARLY = 2
 LEVELS = 5
 OWN = 8 * LEVELS
@@ -49,7 +51,7 @@
     buf, power, inverse, coupled, field, arrive, leave, handed, handing, extra, pair_t, bounce_t,
     load_sem, store_sem, tree_send, tree_recv, cast_send, cast_recv,
     chain_send, chain_recv, hand_send, hand_recv, extra_send, extra_recv, part_send, part_recv,
-    heads, poison, relay_send, relay_recv, give_send, give_recv,
+    heads, poison, relay_send, relay_recv, give_send, give_recv, last_send, last_recv, swap_send, swap_recv,
 ):
     slab = lax.axis_index("slab")
     depth = lax.axis_index("depth")
@@ -74,7 +76,6 @@
 
     rt_x = 1 - core
     qu_x = 2 + core
-    root_z = ROOT_Z
 
     def slot(level, pair, part):
         return level * 8 + pair * 2 + part
@@ -91,18 +92,19 @@
     merged2 = (on_rt & (z2 == 0)) | (on_qu & (z2 == 1))
     inner3 = (on_qu & (z4 == 1)) | (on_rt & (z4 == 2))
     ahead3 = jnp.where(z4 < 2, 1, -1)
-    row = z == root_z
-    root = row & on_rt
-    from_qu = on_qu & (z == root_z + 1)
-    from_rt = on_rt & (z == root_z + 4)
+    near_root, far_root = at(rt_x, NEAR_Z), at(rt_x, FAR_Z)
+    is_near = on_rt & (z == NEAR_Z)
+    is_far = on_rt & (z == FAR_Z)
+    from_qu = on_qu & (z == NEAR_Z + 1)
+    root = is_near | is_far
 
     barrier = pltpu.get_barrier_semaphore()
 
     def greet(**target):
         pl.semaphore_signal(barrier, inc=1, device_id=target, device_id_type=MESH)
 
-    for px, pz in ((1, 0), (-1, 0), (0, 1), (0, -1)):
-        greet(slab=at(x + px, z + pz))
+    for px in (1, 3):
+        greet(slab=at(x + px, z))
     greet(depth=depth + 1 - 2 * core)
 
     @pl.when(y > 0)
@@ -114,10 +116,13 @@
         greet(depth=depth + 2)
 
     meetings = [
-        (from_qu, at(rt_x, root_z)),
-        (from_rt, at(rt_x, root_z)),
-        (root, at(qu_x, root_z + 1)),
-        (root, at(rt_x, root_z + 4)),
+        (from_qu, near_root),
+        (from_qu, far_root),
+        (root, at(qu_x, NEAR_Z + 1)),
+        (is_near, far_root),
+        (is_far, near_root),
+        (z > 0, at(x, z - 1)),
+        (z < 7, at(x, z + 1)),
     ]
     for meets, target in meetings:
 
@@ -126,7 +131,7 @@
             greet(slab=target)
 
     met = [y > 0, y < chips - 1] + [meets for meets, _ in meetings]
-    pl.semaphore_wait(barrier, 5 + sum(flag.astype(jnp.int32) for flag in met))
+    pl.semaphore_wait(barrier, 3 + sum(flag.astype(jnp.int32) for flag in met))
 
     routes = [
         [],
@@ -140,7 +145,8 @@
             (merged2, at(x, z + ahead3), jnp.where(inner3, 2, 0)),
         ],
         [
-            (from_qu | from_rt, at(rt_x, root_z), jnp.where(on_qu, 1, 2)),
+            (from_qu | is_far, near_root, jnp.where(on_qu, 1, 2)),
+            (from_qu | is_near, far_root, jnp.where(on_qu, 1, 0)),
         ],
     ]
     computes = [
@@ -150,7 +156,8 @@
         (on_rt & (z4 == 1)) | (on_qu & (z4 == 2)),
         root,
     ]
-    local = [3, 3, 0, 3, 0]
+    local = [3, 3, 0, 3, 3]
+    holds = [is_near, None, is_far]
 
     def tree_copy(level, number, part, source):
         sends, target, pair = routes[level][number]
@@ -196,14 +203,40 @@
             device_id_type=MESH,
         )
 
+    cut = order // PIECES
+
+    def last_copy(piece):
+        lines = pl.ds(piece * cut, cut)
+        return pltpu.make_async_remote_copy(
+            src_ref=buf.at[OWN + blocks[3], lines],
+            dst_ref=buf.at[TAKEN + blocks[3], lines],
+            send_sem=last_send.at[piece],
+            recv_sem=last_recv.at[piece],
+            device_id={"slab": beside},
+            device_id_type=MESH,
+        )
+
+    def swap_copy(piece):
+        lines = pl.ds(piece * cut, cut)
+        return pltpu.make_async_remote_copy(
+            src_ref=buf.at[slot(0, 3, 0), lines],
+            dst_ref=buf.at[slot(1, 2, 0), lines],
+            send_sem=swap_send.at[piece],
+            recv_sem=swap_recv.at[piece],
+            device_id={"slab": mirror},
+            device_id_type=MESH,
+        )
+
     @pl.when(jnp.logical_not(takes))
     def _():
-        for turn in range(4):
+        for turn in range(3):
             give_copy(turn).start()
+        for piece in range(PIECES):
+            last_copy(piece).start()
 
     head = (pl.ds(0, 8), pl.ds(0, 128))
 
-    def merge(place, wait, finish, transmission_first=False):
+    def merge(place, wait, finish, transmission_first=False, adds=True):
         wait("p1")
         wait("p2")
         near = buf[place["p1"]]
@@ -240,8 +273,11 @@
 
         def reflection():
             wait("m1")
-            wait("add")
-            finish(0, buf[place["add"]] + matmul(buf[place["m1"]], turned))
+            partial = matmul(buf[place["m1"]], turned)
+            if adds:
+                wait("add")
+                partial = buf[place["add"]] + partial
+            finish(0, partial)
 
         def transmission():
             wait("m2")
@@ -275,13 +311,33 @@
     def given(turns):
         def wait(name):
             if name in turns:
-                give_copy(turns[name]).wait_recv()
+                if turns[name] < 3:
+                    give_copy(turns[name]).wait_recv()
+                else:
+                    for piece in range(PIECES):
+                        last_copy(piece).wait_recv()
 
         return wait
 
     def finish_sent(part, value):
         put(slot(0, 3, part), value)
-        send_part(1, part, slot(0, 3, part))
+        if part == 1:
+            send_part(1, 1, slot(0, 3, 1))
+        else:
+            for piece in range(PIECES):
+                swap_copy(piece).start()
+
+    def finish_pieces(part, value):
+        if part == 1:
+            finish_sent(part, value)
+            return
+        put(slot(0, 3, 0), value)
+        addend = sides(x < 2)["add"]
+        for piece in range(PIECES):
+            lines = pl.ds(piece * cut, cut)
+            last_copy(piece).wait_recv()
+            buf[slot(0, 3, 0), lines] += buf[addend, lines]
+            swap_copy(piece).start()
 
     def finish_kept(part, value):
         put(KEPT + part, value)
@@ -293,7 +349,7 @@
 
     @pl.when(takes & (core == 1))
     def _():
-        merge(sides(x < 2), given({"p1": 0, "s": 1, "m1": 2, "add": 3}), finish_sent, transmission_first=True)
+        merge(sides(x < 2), given({"p1": 0, "s": 1, "m1": 2}), finish_pieces, transmission_first=True, adds=False)
         merge(sides(x >= 2), given({}), finish_kept)
 
     names = {"add": (0, 0), "s": (0, 1), "p1": (1, 0), "m1": (1, 1), "p2": (2, 0), "m2": (2, 1)}
@@ -302,11 +358,23 @@
         def operand(pair, part):
             if level == 1:
                 return [KEPT + part, slot(0, 3, part), slot(1, 2, part)][pair]
+            if level == 4:
+                return slot(level, 1, part) if pair == 1 else jnp.where(holds[pair], slot(3, 3, part), slot(level, pair, part))
             return slot(level - 1, 3, part) if local[level] == pair else slot(level, pair, part)
 
         def wait(name):
             pair, part = names[name]
-            if pair == 2 if level == 1 else pair != local[level]:
+            if level == 4 and pair != 1:
+
+                @pl.when(jnp.logical_not(holds[pair]))
+                def _():
+                    await_part(level, pair, part)
+
+                return
+            if level == 1 and name == "p2":
+                for piece in range(PIECES):
+                    swap_copy(piece).wait_recv()
+            elif pair == 2 if level == 1 else pair != local[level]:
                 await_part(level, pair, part)
 
         def finish(part, value):
@@ -324,15 +392,15 @@
             merge_level(level)
 
     dx = lax.rem(x - rt_x + 4, 4)
-    dz = lax.rem(z - root_z + 8, 8)
+    dz = lax.rem(z - NEAR_Z + 4, 4)
     x_first = core == 0
-    x_line = jnp.logical_not(x_first) | row
+    x_line = jnp.logical_not(x_first) | (dz == 0)
     z_line = x_first | (dx == 0)
     children = [
         (x_line & ((dx == 0) | (x_first & (dx == 1))), at(x + 1, z)),
         (x_line & ((dx == 0) | (jnp.logical_not(x_first) & (dx == 3))), at(x - 1, z)),
-        (z_line & (dz <= 3), at(x, z + 1)),
-        (z_line & ((dz == 0) | (dz >= 6)), at(x, z - 1)),
+        (z_line & (dz <= 1), at(x, z + 1)),
+        (z_line & (dz == 0), at(x, z - 1)),
     ]
 
     def cast_copy(which, chunk, child):
@@ -525,12 +593,19 @@
 
     @pl.when(jnp.logical_not(takes))
     def _():
-        for turn in range(4):
+        for turn in range(3):
             give_copy(turn).wait_send()
+        for piece in range(PIECES):
+            last_copy(piece).wait_send()
+
+    @pl.when(takes)
+    def _():
+        for piece in range(PIECES):
+            swap_copy(piece).wait_send()
 
     for level in range(LEVELS):
         for number in range(len(routes[level])):
-            for part in range(2):
+            for part in range(level == 1, 2):
                 sends, copy = tree_copy(level, number, part, OWN)
 
                 @pl.when(sends)
@@ -601,7 +676,7 @@
             dma((CASTS,)), dma((CASTS,)),
             pltpu.VMEM((4, 8, 128), F32), pltpu.VMEM((8, 128), F32),
             dma((2,)), dma((2,)),
-            dma((4,)), dma((4,)),
+            dma((3,)), dma((3,)), dma((PIECES,)), dma((PIECES,)), dma((PIECES,)), dma((PIECES,)),
         ],
         compiler_params=pltpu.CompilerParams(
             collective_id=int(doublings > DOUBLINGS), has_side_effects=True, vmem_limit_bytes=60 * 2**20

time: 268 us -> 257 us (0.959)
  the two profiles are of different devices: /device:TPU:383 before, /device:TPU:63 now
where the time goes in v7:
time: 257 us
  Pallas kernels  254 us (99%)
    pallas_call x2, Pallas kernels, layers(): pl.pallas_call(functools.partial(kernel, doublings), out_shape=(block, bl...  254 us

profile of v7, /device:TPU:63, one launch (start us, length us, event | category | flops | bytes accessed | tf_op | source)
XLA Modules:
  0.0 256.8 jit_solution(13096388864180104250)
XLA Ops:
  0.6 0.0 copy-start
  0.6 0.0 copy-start.1
  0.6 94.9 %layers3.1 = (f32[1,256,256]{2,1,0:T(8,128)S(1)}, f32[1,256,256]{2,1,0:T(8,128)S(1)}, f32[1,1]{1,0:T(1,128)}) custom-call(f32[1,1,4,256,256]{4,3,2,1,0:T(8,128)} %slabs.1, f32[1,256,256]{2,1,0:T(8,128)} %incident.1), custom_call_target="tpu_custom_call" | custom-call | tf_op jit(solution)/shard_map/layers3/pallas_call | solution.py:660
  96.2 0.0 copy-done
  96.2 0.0 copy-done.1
  96.2 159.2 %conditional.1 = ((f32[1,256,256]{2,1,0:T(8,128)S(1)}, f32[1,256,256]{2,1,0:T(8,128)S(1)})) conditional(s32[]{:T(128)} %bitcast, (f32[1,1,4,256,256]{4,3,2,1,0:T(8,128)S(1)}, f32[1,256,256]{2,1,0:T(8,128)S(1)}) %tuple.23, (f32[1,256,256]{2,1,0:T(8,128)S(1)}, f32[1,256,256]{2,1,0:T(8,128)S(1)}) %tuple.15), branch_computations={%region_0.0_spmd, %region_1.0_spmd} | conditional | bytes 24 | solution.py:690
  96.2 159.2 %layers24.1 = (f32[1,256,256]{2,1,0:T(8,128)S(1)}, f32[1,256,256]{2,1,0:T(8,128)S(1)}, f32[1,1]{1,0:T(1,128)}) custom-call(f32[1,1,4,256,256]{4,3,2,1,0:T(8,128)S(1)} %get-tuple-element.8.slabs, f32[1,256,256]{2,1,0:T(8,128)S(1)} %get-tuple-element.9.incident), custom_call_target="tpu_custom_call" | custom-call | tf_op jit(solution)/shard_map/cond/branch_0_fun/layers24/pallas_call | solution.py:660
  255.4 0.7 copy.10
  256.1 0.7 copy.11
Async XLA Ops:
  0.6 95.6 %copy-start = (f32[1,1,4,256,256]{4,3,2,1,0:T(8,128)S(1)}, f32[1,1,4,256,256]{4,3,2,1,0:T(8,128)}, u32[]{:S(2)}) copy-start(f32[1,1,4,256,256]{4,3,2,1,0:T(8,128)} %slabs.1) | copy-start | bytes 3145732
  0.6 95.6 %copy-start.1 = (f32[1,256,256]{2,1,0:T(8,128)S(1)}, f32[1,256,256]{2,1,0:T(8,128)}, u32[]{:S(2)}) copy-start(f32[1,256,256]{2,1,0:T(8,128)} %incident.1) | copy-start | bytes 786436

commit v8 on v7

--- a/solution.py
+++ b/solution.py
@@ -52,6 +52,7 @@
     load_sem, store_sem, tree_send, tree_recv, cast_send, cast_recv,
     chain_send, chain_recv, hand_send, hand_recv, extra_send, extra_recv, part_send, part_recv,
     heads, poison, relay_send, relay_recv, give_send, give_recv, last_send, last_recv, swap_send, swap_recv,
+    final_send, final_recv,
 ):
     slab = lax.axis_index("slab")
     depth = lax.axis_index("depth")
@@ -173,10 +174,28 @@
     def send_part(level, part, source):
         for number in range(len(routes[level])):
             sends, copy = tree_copy(level, number, part, source)
+            if level == 4 and number == 0 and part == 1:
+                sends = from_qu
+
+                @pl.when(is_far)
+                def _():
+                    for piece in range(PIECES):
+                        final_copy(piece).start()
 
             @pl.when(sends)
             def _():
                 copy.start()
+
+    def final_copy(piece):
+        lines = pl.ds(piece * (order // PIECES), order // PIECES)
+        return pltpu.make_async_remote_copy(
+            src_ref=buf.at[slot(3, 3, 1), lines],
+            dst_ref=buf.at[slot(4, 2, 1), lines],
+            send_sem=final_send.at[piece],
+            recv_sem=final_recv.at[piece],
+            device_id={"slab": near_root},
+            device_id_type=MESH,
+        )
 
     def await_part(level, pair, part):
         pltpu.make_async_remote_copy(
@@ -236,7 +255,7 @@
 
     head = (pl.ds(0, 8), pl.ds(0, 128))
 
-    def merge(place, wait, finish, transmission_first=False, adds=True):
+    def merge(place, wait, finish, transmission_first=False, adds=True, stream=None):
         wait("p1")
         wait("p2")
         near = buf[place["p1"]]
@@ -280,6 +299,9 @@
             finish(0, partial)
 
         def transmission():
+            if stream is not None:
+                stream(place["m2"], split(through))
+                return
             wait("m2")
             finish(1, matmul(buf[place["m2"]], through))
 
@@ -352,45 +374,6 @@
         merge(sides(x < 2), given({"p1": 0, "s": 1, "m1": 2}), finish_pieces, transmission_first=True, adds=False)
         merge(sides(x >= 2), given({}), finish_kept)
 
-    names = {"add": (0, 0), "s": (0, 1), "p1": (1, 0), "m1": (1, 1), "p2": (2, 0), "m2": (2, 1)}
-
-    def merge_level(level):
-        def operand(pair, part):
-            if level == 1:
-                return [KEPT + part, slot(0, 3, part), slot(1, 2, part)][pair]
-            if level == 4:
-                return slot(level, 1, part) if pair == 1 else jnp.where(holds[pair], slot(3, 3, part), slot(level, pair, part))
-            return slot(level - 1, 3, part) if local[level] == pair else slot(level, pair, part)
-
-        def wait(name):
-            pair, part = names[name]
-            if level == 4 and pair != 1:
-
-                @pl.when(jnp.logical_not(holds[pair]))
-                def _():
-                    await_part(level, pair, part)
-
-                return
-            if level == 1 and name == "p2":
-                for piece in range(PIECES):
-                    swap_copy(piece).wait_recv()
-            elif pair == 2 if level == 1 else pair != local[level]:
-                await_part(level, pair, part)
-
-        def finish(part, value):
-            put(slot(level, 3, part), value)
-            if level + 1 < LEVELS:
-                send_part(level + 1, part, slot(level, 3, part))
-
-        place = {name: operand(*key) for name, key in names.items()}
-        merge(place, wait, finish, transmission_first=level + 1 == LEVELS)
-
-    for level in range(1, LEVELS):
-
-        @pl.when(computes[level])
-        def _(level=level):
-            merge_level(level)
-
     dx = lax.rem(x - rt_x + 4, 4)
     dz = lax.rem(z - NEAR_Z + 4, 4)
     x_first = core == 0
@@ -424,6 +407,64 @@
             device_id_type=MESH,
         )
 
+    names = {"add": (0, 0), "s": (0, 1), "p1": (1, 0), "m1": (1, 1), "p2": (2, 0), "m2": (2, 1)}
+
+    def merge_level(level):
+        def operand(pair, part):
+            if level == 1:
+                return [KEPT + part, slot(0, 3, part), slot(1, 2, part)][pair]
+            if level == 4:
+                return slot(level, 1, part) if pair == 1 else jnp.where(holds[pair], slot(3, 3, part), slot(level, pair, part))
+            return slot(level - 1, 3, part) if local[level] == pair else slot(level, pair, part)
+
+        def wait(name):
+            pair, part = names[name]
+            if level == 4 and pair != 1:
+
+                @pl.when(jnp.logical_not(holds[pair]))
+                def _():
+                    await_part(level, pair, part)
+
+                return
+            if level == 1 and name == "p2":
+                for piece in range(PIECES):
+                    swap_copy(piece).wait_recv()
+            elif pair == 2 if level == 1 else pair != local[level]:
+                await_part(level, pair, part)
+
+        def finish(part, value):
+            put(slot(level, 3, part), value)
+            if level + 1 < LEVELS:
+                send_part(level + 1, part, slot(level, 3, part))
+
+        def stream(source, right):
+            for piece in range(PIECES):
+                lines = pl.ds(piece * cut, cut)
+
+                @pl.when(is_near)
+                def _():
+                    final_copy(piece).wait_recv()
+
+                buf[FINAL_T, lines] = split_dot(split(buf[source, lines]), right)
+                if piece == 0 and doublings <= DOUBLINGS:
+                    buf[(FINAL_T, *head)] += poison[...]
+                for chunk in range(piece * CASTS // PIECES, (piece + 1) * CASTS // PIECES):
+                    for child in range(4):
+
+                        @pl.when(children[child][0])
+                        def _():
+                            cast_copy(1, chunk, child).start()
+
+        place = {name: operand(*key) for name, key in names.items()}
+        last = level + 1 == LEVELS
+        merge(place, wait, finish, transmission_first=last, stream=stream if last else None)
+
+    for level in range(1, LEVELS):
+
+        @pl.when(computes[level])
+        def _(level=level):
+            merge_level(level)
+
     def relay_copy(way):
         return pltpu.make_async_remote_copy(
             src_ref=heads.at[way],
@@ -460,7 +501,7 @@
 
             for child in range(4):
 
-                @pl.when(children[child][0])
+                @pl.when(children[child][0] & jnp.logical_not(root) if which else children[child][0])
                 def _():
                     cast_copy(which, chunk, child).start()
 
@@ -603,10 +644,17 @@
         for piece in range(PIECES):
             swap_copy(piece).wait_send()
 
+    @pl.when(is_far)
+    def _():
+        for piece in range(PIECES):
+            final_copy(piece).wait_send()
+
     for level in range(LEVELS):
         for number in range(len(routes[level])):
             for part in range(level == 1, 2):
                 sends, copy = tree_copy(level, number, part, OWN)
+                if level == 4 and number == 0 and part == 1:
+                    sends = from_qu
 
                 @pl.when(sends)
                 def _():
@@ -677,6 +725,7 @@
             pltpu.VMEM((4, 8, 128), F32), pltpu.VMEM((8, 128), F32),
             dma((2,)), dma((2,)),
             dma((3,)), dma((3,)), dma((PIECES,)), dma((PIECES,)), dma((PIECES,)), dma((PIECES,)),
+            dma((PIECES,)), dma((PIECES,)),
         ],
         compiler_params=pltpu.CompilerParams(
             collective_id=int(doublings > DOUBLINGS), has_side_effects=True, vmem_limit_bytes=60 * 2**20

time: 257 us -> 255 us (level)
  no operation moved by 1% of the time
where the time goes in v8:
time: 255 us
  Pallas kernels  252 us (99%)
    pallas_call x2, Pallas kernels, layers(): pl.pallas_call(functools.partial(kernel, doublings), out_shape=(block, bl...  252 us

profile of v8, /device:TPU:63, one launch (start us, length us, event | category | flops | bytes accessed | tf_op | source)
XLA Modules:
  0.0 255.1 jit_solution(6880002648293509607)
XLA Ops:
  0.6 0.0 copy-start
  0.6 0.0 copy-start.1
  0.6 93.6 %layers3.1 = (f32[1,256,256]{2,1,0:T(8,128)S(1)}, f32[1,256,256]{2,1,0:T(8,128)S(1)}, f32[1,1]{1,0:T(1,128)}) custom-call(f32[1,1,4,256,256]{4,3,2,1,0:T(8,128)} %slabs.1, f32[1,256,256]{2,1,0:T(8,128)} %incident.1), custom_call_target="tpu_custom_call" | custom-call | tf_op jit(solution)/shard_map/layers3/pallas_call | solution.py:708
  95.0 0.0 copy-done
  95.0 0.0 copy-done.1
  95.0 158.7 %conditional.1 = ((f32[1,256,256]{2,1,0:T(8,128)S(1)}, f32[1,256,256]{2,1,0:T(8,128)S(1)})) conditional(s32[]{:T(128)} %bitcast, (f32[1,1,4,256,256]{4,3,2,1,0:T(8,128)S(1)}, f32[1,256,256]{2,1,0:T(8,128)S(1)}) %tuple.23, (f32[1,256,256]{2,1,0:T(8,128)S(1)}, f32[1,256,256]{2,1,0:T(8,128)S(1)}) %tuple.15), branch_computations={%region_0.0_spmd, %region_1.0_spmd} | conditional | bytes 24 | solution.py:739
  95.0 158.7 %layers24.1 = (f32[1,256,256]{2,1,0:T(8,128)S(1)}, f32[1,256,256]{2,1,0:T(8,128)S(1)}, f32[1,1]{1,0:T(1,128)}) custom-call(f32[1,1,4,256,256]{4,3,2,1,0:T(8,128)S(1)} %get-tuple-element.8.slabs, f32[1,256,256]{2,1,0:T(8,128)S(1)} %get-tuple-element.9.incident), custom_call_target="tpu_custom_call" | custom-call | tf_op jit(solution)/shard_map/cond/branch_0_fun/layers24/pallas_call | solution.py:708
  253.7 0.7 copy.10
  254.4 0.7 copy.11
Async XLA Ops:
  0.6 94.3 %copy-start = (f32[1,1,4,256,256]{4,3,2,1,0:T(8,128)S(1)}, f32[1,1,4,256,256]{4,3,2,1,0:T(8,128)}, u32[]{:S(2)}) copy-start(f32[1,1,4,256,256]{4,3,2,1,0:T(8,128)} %slabs.1) | copy-start | bytes 3145732
  0.6 94.3 %copy-start.1 = (f32[1,256,256]{2,1,0:T(8,128)S(1)}, f32[1,256,256]{2,1,0:T(8,128)}, u32[]{:S(2)}) copy-start(f32[1,256,256]{2,1,0:T(8,128)} %incident.1) | copy-start | bytes 786436

commit v9 on v8

--- a/solution.py
+++ b/solution.py
@@ -18,7 +18,7 @@
 NEAR_Z = 1
 PIECES = 4
 FAR_Z = 5
-EARLY = 2
+EARLY = 1
 LEVELS = 5
 OWN = 8 * LEVELS
 PARTNER = OWN + 4

time: 255 us -> 255 us (level)
  no operation moved by 1% of the time
where the time goes in v9:
time: 255 us
  Pallas kernels  252 us (99%)
    pallas_call x2, Pallas kernels, layers(): pl.pallas_call(functools.partial(kernel, doublings), out_shape=(block, bl...  252 us

profile of v9, /device:TPU:63, one launch (start us, length us, event | category | flops | bytes accessed | tf_op | source)
XLA Modules:
  0.0 255.1 jit_solution(3682265015855306993)
XLA Ops:
  0.6 0.0 copy-start
  0.6 0.0 copy-start.1
  0.6 93.6 %layers3.1 = (f32[1,256,256]{2,1,0:T(8,128)S(1)}, f32[1,256,256]{2,1,0:T(8,128)S(1)}, f32[1,1]{1,0:T(1,128)}) custom-call(f32[1,1,4,256,256]{4,3,2,1,0:T(8,128)} %slabs.1, f32[1,256,256]{2,1,0:T(8,128)} %incident.1), custom_call_target="tpu_custom_call" | custom-call | tf_op jit(solution)/shard_map/layers3/pallas_call | solution.py:708
  95.0 0.0 copy-done
  95.0 0.0 copy-done.1
  95.0 158.7 %conditional.1 = ((f32[1,256,256]{2,1,0:T(8,128)S(1)}, f32[1,256,256]{2,1,0:T(8,128)S(1)})) conditional(s32[]{:T(128)} %bitcast, (f32[1,1,4,256,256]{4,3,2,1,0:T(8,128)S(1)}, f32[1,256,256]{2,1,0:T(8,128)S(1)}) %tuple.23, (f32[1,256,256]{2,1,0:T(8,128)S(1)}, f32[1,256,256]{2,1,0:T(8,128)S(1)}) %tuple.15), branch_computations={%region_0.0_spmd, %region_1.0_spmd} | conditional | bytes 24 | solution.py:739
  95.0 158.7 %layers24.1 = (f32[1,256,256]{2,1,0:T(8,128)S(1)}, f32[1,256,256]{2,1,0:T(8,128)S(1)}, f32[1,1]{1,0:T(1,128)}) custom-call(f32[1,1,4,256,256]{4,3,2,1,0:T(8,128)S(1)} %get-tuple-element.8.slabs, f32[1,256,256]{2,1,0:T(8,128)S(1)} %get-tuple-element.9.incident), custom_call_target="tpu_custom_call" | custom-call | tf_op jit(solution)/shard_map/cond/branch_0_fun/layers24/pallas_call | solution.py:708
  253.7 0.7 copy.10
  254.4 0.7 copy.11
Async XLA Ops:
  0.6 94.3 %copy-start = (f32[1,1,4,256,256]{4,3,2,1,0:T(8,128)S(1)}, f32[1,1,4,256,256]{4,3,2,1,0:T(8,128)}, u32[]{:S(2)}) copy-start(f32[1,1,4,256,256]{4,3,2,1,0:T(8,128)} %slabs.1) | copy-start | bytes 3145732
  0.6 94.3 %copy-start.1 = (f32[1,256,256]{2,1,0:T(8,128)S(1)}, f32[1,256,256]{2,1,0:T(8,128)}, u32[]{:S(2)}) copy-start(f32[1,256,256]{2,1,0:T(8,128)} %incident.1) | copy-start | bytes 786436
